TPU v7x, 128 devices: a whole 4x4x4 slice. The times are simulated.
128 devices in a mesh: gx: 4 (over y), gy: 8 (over z_lo, x), gz: 4 (over z_hi, core).
Axes of the slice: x: 4, y: 4, z: 4 (z_hi: 2, z_lo: 2; z = z_hi * 2 + z_lo), core: 2. Of those that a mesh axis runs over, the one named last changes fastest.
Arguments:
- solution: float32 [16, 64, 128, 512], P(None, 'gx', 'gy', 'gz'), may hold values from -6 to 6
- residual: float32 [16, 64, 128, 512], P(None, 'gx', 'gy', 'gz'), may hold values from -15 to 15, as said below
- direction: float32 [16, 64, 128, 512], P(None, 'gx', 'gy', 'gz'), may hold values from -13 to 13, as said below
- kappa_squared: float32 [64, 128, 512], P('gx', 'gy', 'gz'), may hold values from 0.02 to 0.2
- conductance: float32 [64, 128, 512], P('gx', 'gy', 'gz'), may hold values from 0.1 to 1
Outputs:
- new_solution: float32 [16, 64, 128, 512], P(None, 'gx', 'gy', 'gz')
- new_residual: float32 [16, 64, 128, 512], P(None, 'gx', 'gy', 'gz')
- new_direction: float32 [16, 64, 128, 512], P(None, 'gx', 'gy', 'gz')
Inputs may be any that keep to these rules, and one draw needn't show every extreme that they name: residual is drawn with a part that is independent for each sample and each cell. direction is correlated with residual, sample by sample.
All inputs are finite; a program needn't handle non-finite values.
Results may differ from a plain program's by a relative error of at most 0.0003.
Values sent between devices are 32-bit elements; how exact they have to be, the bound alone decides.
No kernel may reach another device: no remote copies, remote signals or barrier semaphores. Data moves between devices by JAX's collectives and lax.ppermute only.
A program may use at most 128 MiB of HBM per device.

v0:
```python
import jax
import jax.numpy as jnp
from jax import lax
from jax.sharding import PartitionSpec as P

ITERS = 2


def with_halo(block, sides, width):
    for axis, dim in sides:
        count = lax.axis_size(axis)
        forward = [(i, i + 1) for i in range(count - 1)]
        backward = [(target, source) for source, target in forward]
        low = lax.ppermute(
            lax.slice_in_dim(block, block.shape[dim] - width, None, axis=dim), axis, forward
        )
        high = lax.ppermute(lax.slice_in_dim(block, 0, width, axis=dim), axis, backward)
        block = jnp.concatenate([low, block, high], axis=dim)
    return block


def six_sides(array):
    return [
        array[..., 2:, 1:-1, 1:-1],
        array[..., :-2, 1:-1, 1:-1],
        array[..., 1:-1, 2:, 1:-1],
        array[..., 1:-1, :-2, 1:-1],
        array[..., 1:-1, 1:-1, 2:],
        array[..., 1:-1, 1:-1, :-2],
    ]


def laplace(padded, kappa, conduct):
    centre = padded[..., 1:-1, 1:-1, 1:-1]
    conduct_mid = conduct[1:-1, 1:-1, 1:-1]
    total = kappa * centre
    for beside, face_dif in zip(six_sides(padded), six_sides(conduct)):
        total = total + 0.5 * (conduct_mid + face_dif) * (centre - beside)
    return total


def local_gram(first, second, count):
    return (
        jnp.dot(
            first.reshape(first.shape[0], -1),
            second.reshape(second.shape[0], -1).T,
            precision=lax.Precision.HIGHEST,
        )
        / count
    )


def symmetric(matrix):
    return 0.5 * (matrix + matrix.T)


def spd_solve(matrix, right):
    factor = jnp.linalg.cholesky(matrix)
    inner = lax.linalg.triangular_solve(factor, right, left_side=True, lower=True)
    return lax.linalg.triangular_solve(factor, inner, left_side=True, lower=True, transpose_a=True)


def combine(matrix, fields):
    flat = fields.reshape(fields.shape[0], -1)
    return jnp.dot(matrix, flat, precision=lax.Precision.HIGHEST).reshape(fields.shape)


def single_pass(field, kappa, conduct):
    padded = with_halo(field, (("gx", 1), ("gy", 2), ("gz", 3)), 1)
    return laplace(padded, kappa, conduct)


def body(solution, residual, direction, kappa_squared, conductance):
    samples, cells_x, cells_y, cells_z = direction.shape
    devices_all = lax.axis_size("gx") * lax.axis_size("gy") * lax.axis_size("gz")
    count = jnp.float32(cells_x * cells_y * cells_z * devices_all)
    coefs = with_halo(jnp.stack([kappa_squared, conductance]), (("gx", 1), ("gy", 2), ("gz", 3)), 2)
    kappa_mid = coefs[0, 2:-2, 2:-2, 2:-2]
    conduct_one = coefs[1, 1:-1, 1:-1, 1:-1]
    identity = jnp.eye(samples, dtype=jnp.float32)
    for iteration in range(ITERS):
        middle = single_pass(direction, kappa_mid, conduct_one)
        image = single_pass(middle, kappa_mid, conduct_one)
        dir_img, dir_res = lax.psum(
            (local_gram(direction, image, count), local_gram(direction, residual, count)),
            ("gx", "gy", "gz"),
        )
        curvature = symmetric(dir_img)
        step_mat = spd_solve(curvature, dir_res)
        solution = solution + combine(step_mat.T, direction)
        residual = residual - combine(step_mat.T, image)
        img_new = lax.psum(local_gram(image, residual, count), ("gx", "gy", "gz"))
        correction = -spd_solve(curvature, img_new)
        fresh = residual + combine(correction.T, direction)
        norms_mat = lax.psum(local_gram(fresh, fresh, count), ("gx", "gy", "gz"))
        factor = jnp.linalg.cholesky(symmetric(norms_mat))
        inverse = lax.linalg.triangular_solve(factor, identity, left_side=True, lower=True)
        direction = combine(inverse, fresh)
    return (solution, residual, direction)


def solution(mesh):
    in_specs = (
        P(None, "gx", "gy", "gz"),
        P(None, "gx", "gy", "gz"),
        P(None, "gx", "gy", "gz"),
        P("gx", "gy", "gz"),
        P("gx", "gy", "gz"),
    )
    out_specs = (P(None, "gx", "gy", "gz"), P(None, "gx", "gy", "gz"), P(None, "gx", "gy", "gz"))
    return jax.shard_map(body, mesh=mesh, in_specs=in_specs, out_specs=out_specs, check_vma=False)
```

profile of v0, /device:TPU:1, one launch (start us, length us, event | category | flops | bytes accessed | tf_op | source)
XLA Modules:
  0.0 766.6 jit_solution(1931507717396356238)
XLA Ops:
  27.1 4.6 collective-permute-start.9
  32.0 9.8 %collective-permute-start.4 = (f32[2,20,20,2]{3,2,1,0:T(8,128)S(1)}, f32[2,20,20,2]{3,2,1,0:T(8,128)S(1)}, u32[]{:S(2)}, u32[]{:S(2)}) collective-permute-start(f32[2,20,20,2]{3,2,1,0:T(8,128)S(1)} %get-tuple-element.58), channel_id=1, source_target_pairs={{0,1},{1,2},{2,3},{4,5},{5,6},{6,7},{8,9},{9,10},{10,11},{12,13},{... | collective-permute-start | bytes 19208 | tf_op jit(solution)/shard_map/ppermute | solution.py:14
  43.7 4.8 collective-permute-done.4
  48.5 4.9 collective-permute-done.5
  69.7 5.1 collective-permute-start.11
  83.2 8.6 %fusion.64 = f32[16,16,16,128]{3,2,1,0:T(8,128)S(1)} fusion(f32[16,16,16,128]{3,2,1,0:T(8,128)S(1)} %copy-done, f32[16,18,18,1]{3,2,1,0:T(8,128)} %copy.549, f32[16,18,1,128]{3,2,1,0:T(1,128)S(1)} %copy-done.20, f32[16,18,16,128]{3,2,1,0:T(8,128)} %copy-done.13, f32[16,18,1,128]{3,2,1,0:T(1,128)S(1)} %copy-done.22, f32[16,18,18,1]{3,2,1,0:T(8,128)} %copy.547, ...), kind=kLoop, calls=%fused_computation.119 | loop fusion | flops 15204352 | bytes 8069632 | tf_op jit(solution)/shard_map/add | solution.py:38
  122.9 5.1 collective-permute-start.17
  128.0 6.3 fusion.139
  145.7 12.2 %fusion.46 = f32[16,16,16,128]{3,2,1,0:T(8,128)S(1)} fusion(f32[16,16,16,128]{3,2,1,0:T(8,128)} %copy-done.4, f32[16,18,18,1]{3,2,1,0:T(8,128)} %copy.559, f32[16,18,1,128]{3,2,1,0:T(1,128)S(1)} %copy.551, f32[16,18,1,128]{3,2,1,0:T(1,128)S(1)} %copy.553, f32[16,1,16,128]{3,2,1,0:T(8,128)S(1)} %collective-permute-done.12, f32[16,1,16,128]{3,2,1,0:T(8,128)} %copy-done.24, ...), kind=kLoop, calls=%fused_computation.83 | loop fusion | flops 19398656 | bytes 5710336 | tf_op jit(solution)/shard_map/add | solution.py:38
  157.9 4.8 fusion.149
  165.7 72.3 %all-reduce.1 = (f32[16,16]{1,0:T(8,128)S(1)}, f32[16,16]{0,1:T(8,128)S(1)}) all-reduce(f32[16,16]{1,0:T(8,128)S(1)} %fusion.139, f32[16,16]{0,1:T(8,128)S(1)} %fusion.149), channel_id=1, replica_groups=mesh['gx'=4,'gy'=8,'gz'=4] {'gx','gy','gz'}, use_global_device_ids=true, to_apply=%region_3.0 | all-reduce | flops 512 | bytes 4096 | tf_op jit(solution)/shard_map/psum | solution.py:84
  242.5 6.2 copy_subtract_fusion
  252.3 62.8 %psum.58 = f32[16,16]{1,0:T(8,128)S(1)} all-reduce(f32[16,16]{1,0:T(8,128)S(1)} %fusion.154), channel_id=1, replica_groups=mesh['gx'=4,'gy'=8,'gz'=4] {'gx','gy','gz'}, use_global_device_ids=true, to_apply=%region_4.8 | all-reduce | flops 256 | bytes 2048 | tf_op jit(solution)/shard_map/psum | solution.py:92
  324.6 64.3 %psum.59 = f32[16,16]{1,0:T(8,128)S(1)} all-reduce(f32[16,16]{1,0:T(8,128)S(1)} %fusion.134), channel_id=1, replica_groups=mesh['gx'=4,'gy'=8,'gz'=4] {'gx','gy','gz'}, use_global_device_ids=true, to_apply=%region_5.9 | all-reduce | flops 256 | bytes 2048 | tf_op jit(solution)/shard_map/psum | solution.py:95
  422.3 5.1 collective-permute-start.22
  442.6 9.5 %fusion.28 = f32[16,16,16,128]{3,2,1,0:T(8,128)S(1)} fusion(f32[16,16,16,128]{3,2,1,0:T(8,128)} %bitcast.244, f32[16,18,18,1]{3,2,1,0:T(8,128)} %copy.589, f32[16,18,1,128]{3,2,1,0:T(1,128)S(1)} %copy.581, f32[16,18,16,128]{3,2,1,0:T(8,128)} %copy-done.14, f32[16,18,1,128]{3,2,1,0:T(1,128)S(1)} %copy.583, f32[16,18,18,1]{3,2,1,0:T(8,128)} %copy.587, ...), kind=kLoop, calls=%fused_computation.55 | loop fusion | flops 15204352 | bytes 8069632 | tf_op jit(solution)/shard_map/add | solution.py:38
  461.8 4.7 collective-permute-start.27
  489.0 5.0 fusion.130
  502.1 11.4 %fusion.10 = f32[16,16,16,128]{3,2,1,0:T(8,128)S(1)} fusion(f32[16,16,16,128]{3,2,1,0:T(8,128)} %copy-done.3, f32[16,18,18,1]{3,2,1,0:T(8,128)} %copy.599, f32[16,18,1,128]{3,2,1,0:T(1,128)S(1)} %copy.591, f32[16,18,1,128]{3,2,1,0:T(1,128)S(1)} %copy.593, f32[16,1,16,128]{3,2,1,0:T(8,128)S(1)} %collective-permute-done.24, f32[16,1,16,128]{3,2,1,0:T(8,128)} %copy-done.23, ...), kind=kLoop, calls=%fused_computation.19 | loop fusion | flops 19398656 | bytes 5710336 | tf_op jit(solution)/shard_map/add | solution.py:38
  520.1 70.6 %all-reduce = (f32[16,16]{1,0:T(8,128)S(1)}, f32[16,16]{1,0:T(8,128)S(1)}) all-reduce(f32[16,16]{1,0:T(8,128)S(1)} %fusion.130, f32[16,16]{1,0:T(8,128)S(1)} %fusion.127), channel_id=1, replica_groups=mesh['gx'=4,'gy'=8,'gz'=4] {'gx','gy','gz'}, use_global_device_ids=true, to_apply=%region_7.11 | all-reduce | flops 512 | bytes 4096 | tf_op jit(solution)/shard_map/psum | solution.py:84
  595.3 5.2 fusion.108
  605.4 64.2 %psum.62 = f32[16,16]{1,0:T(8,128)S(1)} all-reduce(f32[16,16]{1,0:T(8,128)S(1)} %fusion.136), channel_id=1, replica_groups=mesh['gx'=4,'gy'=8,'gz'=4] {'gx','gy','gz'}, use_global_device_ids=true, to_apply=%region_8.12 | all-reduce | flops 256 | bytes 2048 | tf_op jit(solution)/shard_map/psum | solution.py:92
  685.2 62.7 %psum.63 = f32[16,16]{1,0:T(8,128)S(1)} all-reduce(f32[16,16]{1,0:T(8,128)S(1)} %fusion.133), channel_id=1, replica_groups=mesh['gx'=4,'gy'=8,'gz'=4] {'gx','gy','gz'}, use_global_device_ids=true, to_apply=%region_9.13 | all-reduce | flops 256 | bytes 2048 | tf_op jit(solution)/shard_map/psum | solution.py:95
  759.4 5.0 copy_add_fusion.1
  (247 shorter events, 249.5 us)
Async XLA Ops:
  11.2 9.9 %collective-permute-start.2 = (f32[2,20,2,128]{3,2,1,0:T(2,128)S(1)}, f32[2,20,2,128]{3,2,1,0:T(2,128)S(1)}, u32[]{:S(2)}, u32[]{:S(2)}) collective-permute-start(f32[2,20,2,128]{3,2,1,0:T(2,128)S(1)} %get-tuple-element.66), channel_id=1, source_target_pairs={{0,4},{4,8},{8,12},{12,16},{16,20},{20,24},{24,28},{1,5},{5,9},{9,... | collective-permute-start | bytes 122888 | tf_op jit(solution)/shard_map/ppermute | solution.py:14
  14.3 6.8 collective-permute-start.3
  19.9 5.7 collective-permute-start.6
  25.8 28.0 %collective-permute-start.8 = (f32[16,18,1,128]{3,0,2,1:T(8,128)S(1)}, f32[16,18,1,128]{3,0,2,1:T(8,128)S(1)}, u32[]{:S(2)}, u32[]{:S(2)}) collective-permute-start(f32[16,18,1,128]{3,0,2,1:T(8,128)S(1)} %copy.630), channel_id=1, source_target_pairs={{4,0},{8,4},{12,8},{16,12},{20,16},{24,20},{28,24},{5,1},{9,5},{13... | collective-permute-start | bytes 442376 | tf_op jit(solution)/shard_map/ppermute | solution.py:17
  27.1 26.8 %collective-permute-start.9 = (f32[16,18,1,128]{3,0,2,1:T(8,128)S(1)}, f32[16,18,1,128]{3,0,2,1:T(8,128)S(1)}, u32[]{:S(2)}, u32[]{:S(2)}) collective-permute-start(f32[16,18,1,128]{3,0,2,1:T(8,128)S(1)} %copy.631), channel_id=1, source_target_pairs={{0,4},{4,8},{8,12},{12,16},{16,20},{20,24},{24,28},{1,5},{5,9},{9,... | collective-permute-start | bytes 442376 | tf_op jit(solution)/shard_map/ppermute | solution.py:14
  32.0 16.5 %collective-permute-start.4 = (f32[2,20,20,2]{3,2,1,0:T(8,128)S(1)}, f32[2,20,20,2]{3,2,1,0:T(8,128)S(1)}, u32[]{:S(2)}, u32[]{:S(2)}) collective-permute-start(f32[2,20,20,2]{3,2,1,0:T(8,128)S(1)} %get-tuple-element.58), channel_id=1, source_target_pairs={{0,1},{1,2},{2,3},{4,5},{5,6},{6,7},{8,9},{9,10},{10,11},{12,13},{... | collective-permute-start | bytes 19208 | tf_op jit(solution)/shard_map/ppermute | solution.py:14
  41.7 11.7 %collective-permute-start.5 = (f32[2,20,20,2]{3,2,1,0:T(8,128)S(1)}, f32[2,20,20,2]{3,2,1,0:T(8,128)S(1)}, u32[]{:S(2)}, u32[]{:S(2)}) collective-permute-start(f32[2,20,20,2]{3,2,1,0:T(8,128)S(1)} %get-tuple-element.59), channel_id=1, source_target_pairs={{1,0},{2,1},{3,2},{5,4},{6,5},{7,6},{9,8},{10,9},{11,10},{13,12},{... | collective-permute-start | bytes 19208 | tf_op jit(solution)/shard_map/ppermute | solution.py:17
  63.8 11.3 %collective-permute-start.10 = (f32[16,18,18,1]{2,0,3,1:T(8,128)}, f32[16,18,18,1]{2,0,3,1:T(8,128)}, u32[]{:S(2)}, u32[]{:S(2)}) collective-permute-start(f32[16,18,18,1]{2,0,3,1:T(8,128)} %copy.546), channel_id=1, source_target_pairs={{1,0},{2,1},{3,2},{5,4},{6,5},{7,6},{9,8},{10,9},{11,10},{13,12},{... | collective-permute-start | bytes 62216 | tf_op jit(solution)/shard_map/ppermute | solution.py:17
  69.7 9.4 %collective-permute-start.11 = (f32[16,18,18,1]{2,0,3,1:T(8,128)}, f32[16,18,18,1]{2,0,3,1:T(8,128)}, u32[]{:S(2)}, u32[]{:S(2)}) collective-permute-start(f32[16,18,18,1]{2,0,3,1:T(8,128)} %copy.548), channel_id=1, source_target_pairs={{0,1},{1,2},{2,3},{4,5},{5,6},{6,7},{8,9},{9,10},{10,11},{12,13},{... | collective-permute-start | bytes 62216 | tf_op jit(solution)/shard_map/ppermute | solution.py:14
  93.1 6.0 collective-permute-start.13
  99.3 7.0 collective-permute-start.14
  100.7 7.4 collective-permute-start.15
  116.8 20.5 %collective-permute-start.16 = (f32[16,18,18,1]{2,0,3,1:T(8,128)}, f32[16,18,18,1]{2,0,3,1:T(8,128)}, u32[]{:S(2)}, u32[]{:S(2)}) collective-permute-start(f32[16,18,18,1]{2,0,3,1:T(8,128)} %copy.556), channel_id=1, source_target_pairs={{1,0},{2,1},{3,2},{5,4},{6,5},{7,6},{9,8},{10,9},{11,10},{13,12},{... | collective-permute-start | bytes 62216 | tf_op jit(solution)/shard_map/ppermute | solution.py:17
  122.9 18.8 %collective-permute-start.17 = (f32[16,18,18,1]{2,0,3,1:T(8,128)}, f32[16,18,18,1]{2,0,3,1:T(8,128)}, u32[]{:S(2)}, u32[]{:S(2)}) collective-permute-start(f32[16,18,18,1]{2,0,3,1:T(8,128)} %copy.558), channel_id=1, source_target_pairs={{0,1},{1,2},{2,3},{4,5},{5,6},{6,7},{8,9},{9,10},{10,11},{12,13},{... | collective-permute-start | bytes 62216 | tf_op jit(solution)/shard_map/ppermute | solution.py:14
  399.4 5.9 collective-permute-start.18
  406.2 5.9 collective-permute-start.20
  422.3 12.2 %collective-permute-start.22 = (f32[16,18,18,1]{2,0,3,1:T(8,128)}, f32[16,18,18,1]{2,0,3,1:T(8,128)}, u32[]{:S(2)}, u32[]{:S(2)}) collective-permute-start(f32[16,18,18,1]{2,0,3,1:T(8,128)} %copy.586), channel_id=1, source_target_pairs={{1,0},{2,1},{3,2},{5,4},{6,5},{7,6},{9,8},{10,9},{11,10},{13,12},{... | collective-permute-start | bytes 62216 | tf_op jit(solution)/shard_map/ppermute | solution.py:17
  431.4 7.1 collective-permute-start.23
  452.1 7.2 collective-permute-start.24
  453.7 6.5 collective-permute-start.25
  460.5 8.0 %collective-permute-start.26 = (f32[16,18,1,128]{3,0,2,1:T(8,128)S(1)}, f32[16,18,1,128]{3,0,2,1:T(8,128)S(1)}, u32[]{:S(2)}, u32[]{:S(2)}) collective-permute-start(f32[16,18,1,128]{3,0,2,1:T(8,128)S(1)} %copy.590), channel_id=1, source_target_pairs={{4,0},{8,4},{12,8},{16,12},{20,16},{24,20},{28,24},{5,1},{9,5},{13... | collective-permute-start | bytes 442376 | tf_op jit(solution)/shard_map/ppermute | solution.py:17
  461.8 6.9 collective-permute-start.27
  477.4 16.7 %collective-permute-start.28 = (f32[16,18,18,1]{2,0,3,1:T(8,128)}, f32[16,18,18,1]{2,0,3,1:T(8,128)}, u32[]{:S(2)}, u32[]{:S(2)}) collective-permute-start(f32[16,18,18,1]{2,0,3,1:T(8,128)} %copy.596), channel_id=1, source_target_pairs={{1,0},{2,1},{3,2},{5,4},{6,5},{7,6},{9,8},{10,9},{11,10},{13,12},{... | collective-permute-start | bytes 62216 | tf_op jit(solution)/shard_map/ppermute | solution.py:17
  485.2 12.9 %collective-permute-start.29 = (f32[16,18,18,1]{2,0,3,1:T(8,128)}, f32[16,18,18,1]{2,0,3,1:T(8,128)}, u32[]{:S(2)}, u32[]{:S(2)}) collective-permute-start(f32[16,18,18,1]{2,0,3,1:T(8,128)} %copy.598), channel_id=1, source_target_pairs={{0,1},{1,2},{2,3},{4,5},{5,6},{6,7},{8,9},{9,10},{10,11},{12,13},{... | collective-permute-start | bytes 62216 | tf_op jit(solution)/shard_map/ppermute | solution.py:14
  (35 other events, 355.6 us)
where the time goes:
time: 777 us; the launch traced here: 767 us
  blocking collectives  397 us (51%)
  local copies, waits for them, and re-layouts  113 us (15%)
  starting transfers between devices  92.2 us (12%)
  matrix products  67.4 us (9%)
  other arithmetic  65.2 us (8%)
  waiting for transfers between devices  29.5 us (4%)
    psum x2, blocking collectives, body(): lax.psum((local_gram(direction, image, count), local_gram(direction, resi...  143 us
    psum x2, blocking collectives, body(): norms_mat = lax.psum(local_gram(fresh, fresh, count), ('gx', 'gy', 'gz'))  127 us
    psum x2, blocking collectives, body(): img_new = lax.psum(local_gram(image, residual, count), ('gx', 'gy', 'gz'))  127 us
    ppermute x15, starting transfers between devices, with_halo(): lax.ppermute(lax.slice_in_dim(block, block.shape[dim] - width, None, axis...  63.7 us
    add x4, other arithmetic, laplace(): total = total + 0.5 * (conduct_mid + face_dif) * (centre - beside)  41.7 us
    dot_general x8, matrix products, combine(): jnp.dot(matrix, flat, precision=lax.Precision.HIGHEST).reshape(fields.shape)  33.2 us
    slice x12, local copies, waits for them, and re-layouts, with_halo(): lax.slice_in_dim(block, 0, width, axis=dim)  32.8 us
    dot_general x8, matrix products, local_gram(): jnp.dot(first.reshape(first.shape[0], -1), second.reshape(second.shape[0]...  32.4 us
  transfers between devices with their start and end apart: 30, of which 14 were waited for; matrix products, arithmetic and copies ran while one was open for 7% of the time, Pallas kernels for 0%

commit v1 on v0

v1 whole, which is shorter than its diff:
```python
import functools

import jax
import jax.numpy as jnp
from jax import lax
from jax.experimental import pallas as pl
from jax.experimental.pallas import tpu as pltpu
from jax.sharding import PartitionSpec as P

AXES = ("gx", "gy", "gz")
S = 16
NX, NY, NZ = 16, 16, 128
F32, BF16 = jnp.float32, jnp.bfloat16
VMEM = pl.BlockSpec(memory_space=pltpu.VMEM)
PARAMS = pltpu.CompilerParams(vmem_limit_bytes=56 << 20)


def lanes(shape):
    return lax.broadcasted_iota(jnp.int32, shape, len(shape) - 1)


def lane_roll(v, shift):
    return pltpu.roll(v, shift, v.ndim - 1)


def put_z_face(ref, row, acc, off, lane):
    moved = lane_roll(acc, off)
    ref[row] = jnp.where((lane >= off) & (lane < off + NY), moved, ref[row])


def enter_kernel(d_ref, r_ref, c_ref, out_ref, xl, xh, yl, yh, zl, zh):
    x = pl.program_id(0)
    lane = lanes((S, NZ))
    off = lax.rem(x, 8) * NY
    for f, ref in enumerate((d_ref, r_ref)):
        flat = ref.reshape(S * NY, NZ)
        accl = jnp.zeros((S, NZ), F32)
        acch = jnp.zeros((S, NZ), F32)
        for y in range(NY):
            v = flat[pl.ds(y, S, stride=NY), :]
            out_ref[f, 0, y] = v
            accl = jnp.where(lane == y, lane_roll(v, y) if y else v, accl)
            acch = jnp.where(lane == y, lane_roll(v, y + 1), acch)
            if y == 0:
                yl[f * NX + x] = v
            if y == NY - 1:
                yh[f * NX + x] = v
        put_z_face(zl, f * 2 + x // 8, accl, off, lane)
        put_z_face(zh, f * 2 + x // 8, acch, off, lane)

    cond = c_ref[0]
    yl[2 * NX, pl.ds(x, 1), :] = cond[0:1]
    yh[2 * NX, pl.ds(x, 1), :] = cond[NY - 1 : NY]
    zl[4] = jnp.where(lane == x, lane_roll(cond, x), zl[4])
    zh[4] = jnp.where(lane == x, lane_roll(cond, x + 1), zh[4])

    @pl.when(x == 0)
    def _():
        for f in range(2):
            for y in range(NY):
                xl[f * NY + y] = out_ref[f, 0, y]
        xl[2 * NY] = cond

    @pl.when(x == NX - 1)
    def _():
        for f in range(2):
            for y in range(NY):
                xh[f * NY + y] = out_ref[f, 0, y]
        xh[2 * NY] = cond


def enter(direction, residual, conductance):
    block = pl.BlockSpec((S, 1, NY, NZ), lambda x: (0, x, 0, 0))
    whole = lambda n: pl.BlockSpec((n, S, NZ), lambda x: (0, 0, 0))
    shape = lambda n: jax.ShapeDtypeStruct((n, S, NZ), F32)
    rows = (33, 33, 33, 33, 5, 5)
    return pl.pallas_call(
        enter_kernel,
        grid=(NX,),
        in_specs=[block, block, pl.BlockSpec((1, NY, NZ), lambda x: (x, 0, 0))],
        out_specs=[pl.BlockSpec((2, 1, NY, S, NZ), lambda x: (0, x, 0, 0, 0))] + [whole(n) for n in rows],
        out_shape=[jax.ShapeDtypeStruct((2, NX, NY, S, NZ), F32)] + [shape(n) for n in rows],
        name="enter",
    )(direction, residual, conductance)


def coef_kernel(flag, kappa, cond, xl, xh, yl, yh, zl, zh, out):
    lane = lanes((NY, NZ))
    sub = lax.broadcasted_iota(jnp.int32, (NY, NZ), 0)

    def per_x(x, _):
        c = cond[x]
        prev = jnp.where(x == 0, xl[2 * NY] * flag[0], cond[jnp.maximum(x - 1, 0)])
        nxt = jnp.where(x == NX - 1, xh[2 * NY] * flag[1], cond[jnp.minimum(x + 1, NX - 1)])
        ylo = yl[2 * NX, pl.ds(x, 1), :] * flag[2]
        yhi = yh[2 * NX, pl.ds(x, 1), :] * flag[3]
        ym = jnp.where(sub == 0, ylo, pltpu.roll(c, 1, 0))
        yp = jnp.where(sub == NY - 1, yhi, pltpu.roll(c, NY - 1, 0))
        zlo = lane_roll(zl[4], lax.rem(NZ - x, NZ)) * flag[4]
        zhi = lane_roll(zh[4], NZ - 1 - x) * flag[5]
        zm = jnp.where(lane == 0, zlo, lane_roll(c, 1))
        zp = jnp.where(lane == NZ - 1, zhi, lane_roll(c, NZ - 1))
        g = [0.5 * (c + n) for n in (prev, nxt, ym, yp, zm, zp)]
        out[0, x] = kappa[x] + ((g[0] + g[1]) + (g[2] + g[3]) + (g[4] + g[5]))
        out[1, x] = jnp.where(x == 0, g[0] * flag[0], g[0])
        out[2, x] = jnp.where(x == NX - 1, g[1] * flag[1], g[1])
        out[3, x] = jnp.where(sub == 0, g[2] * flag[2], g[2])
        out[4, x] = jnp.where(sub == NY - 1, g[3] * flag[3], g[3])
        out[5, x] = jnp.where(lane == 0, g[4] * flag[4], g[4])
        out[6, x] = jnp.where(lane == NZ - 1, g[5] * flag[5], g[5])
        return 0

    lax.fori_loop(0, NX, per_x, 0)


def coefs(flags, kappa, cond, halos):
    return pl.pallas_call(
        coef_kernel,
        in_specs=[pl.BlockSpec(memory_space=pltpu.SMEM)] + [VMEM] * 8,
        out_specs=VMEM,
        out_shape=jax.ShapeDtypeStruct((7, NX, NY, NZ), F32),
        compiler_params=PARAMS,
        name="coefs",
    )(flags, kappa, cond, *halos)


def stencil_kernel(nf, ne, field, xl, xh, yl, yh, zl, zh, coef, out, *faces):
    lane = lanes((S, NZ))
    first, last = lane == 0, lane == NZ - 1
    if ne:
        oxl, oxh, oyl, oyh, ozl, ozh = faces

    def per_x(x, edge):
        off = lax.rem(x, 8) * NY
        back = lax.rem(NZ - off, NZ)
        half = x // 8
        zlo = [lane_roll(zl[f * 2 + half], back) for f in range(nf)]
        zhi = [lane_roll(zh[f * 2 + half], back) for f in range(nf)]
        accl = [jnp.zeros((S, NZ), F32) for _ in range(ne)]
        acch = [jnp.zeros((S, NZ), F32) for _ in range(ne)]
        for y in range(NY):
            k = [jnp.broadcast_to(coef[i, x, y : y + 1, :], (S, NZ)) for i in range(7)]
            for f in range(nf):
                c = field[f, x, y]
                xm = xl[f * NY + y] if edge == "lo" else field[f, x - 1, y]
                xp = xh[f * NY + y] if edge == "hi" else field[f, x + 1, y]
                ym = field[f, x, y - 1] if y else yl[f * NX + x]
                yp = field[f, x, y + 1] if y < NY - 1 else yh[f * NX + x]
                zm = jnp.where(first, lane_roll(zlo[f], (NZ - y) % NZ) if y else zlo[f], lane_roll(c, 1))
                zp = jnp.where(last, lane_roll(zhi[f], NZ - 1 - y), lane_roll(c, NZ - 1))
                o = ((k[0] * c - k[1] * xm) - (k[2] * xp + k[3] * ym)) - ((k[4] * yp + k[5] * zm) + k[6] * zp)
                out[f, x, y] = o
                if f < ne:
                    accl[f] = jnp.where(lane == y, lane_roll(o, y) if y else o, accl[f])
                    acch[f] = jnp.where(lane == y, lane_roll(o, y + 1), acch[f])
                    if edge == "lo":
                        oxl[f * NY + y] = o
                    if edge == "hi":
                        oxh[f * NY + y] = o
                    if y == 0:
                        oyl[f * NX + x] = o
                    if y == NY - 1:
                        oyh[f * NX + x] = o
        for f in range(ne):
            put_z_face(ozl, f * 2 + half, accl[f], off, lane)
            put_z_face(ozh, f * 2 + half, acch[f], off, lane)

    per_x(jnp.int32(0), "lo")
    lax.fori_loop(1, NX - 1, lambda x, c: (per_x(x, ""), c)[1], 0)
    per_x(jnp.int32(NX - 1), "hi")


def stencil(field, halos, coef, nf, ne):
    shape = lambda n: jax.ShapeDtypeStruct((n, S, NZ), F32)
    faces = [shape(n) for n in (16 * ne, 16 * ne, 16 * ne, 16 * ne, 2 * ne, 2 * ne)] if ne else []
    return pl.pallas_call(
        functools.partial(stencil_kernel, nf, ne),
        in_specs=[VMEM] * 8,
        out_specs=[VMEM] * (1 + len(faces)),
        out_shape=[jax.ShapeDtypeStruct((nf, NX, NY, S, NZ), F32)] + faces,
        compiler_params=PARAMS,
        name=f"stencil{nf}{ne}",
    )(field, *halos, coef)


def exchange(faces):
    halos = []
    for i, axis in enumerate(AXES):
        n = lax.axis_size(axis)
        low, high = faces[2 * i], faces[2 * i + 1]
        halos.append(lax.ppermute(high, axis, [(j, (j + 1) % n) for j in range(n)]))
        halos.append(lax.ppermute(low, axis, [(j, (j - 1) % n) for j in range(n)]))
    return halos


def gram_kernel(dr, qw, z, halves, gram, acc):
    x = pl.program_id(0)
    fields = (dr.at[0, 0], qw.at[0, 0], dr.at[1, 0], qw.at[1, 0], z.at[0, 0])
    for y in range(NY):
        for i, ref in enumerate(fields):
            v = ref[y]
            hi = v.astype(BF16)
            halves[y, 16 * i : 16 * i + 16, :] = hi
            halves[y, 80 + 16 * i : 96 + 16 * i, :] = (v - hi.astype(F32)).astype(BF16)
    op = jnp.concatenate([halves[y] for y in range(NY)], axis=1)
    part = lax.dot_general(op, op, (((1,), (1,)), ((), ())), preferred_element_type=F32)

    @pl.when(x == 0)
    def _():
        acc[...] = part

    @pl.when(x > 0)
    def _():
        acc[...] = acc[...] + part

    @pl.when(x == NX - 1)
    def _():
        a = acc[...]
        rows = a[:80] + a[80:]
        left, right = rows[:, :128], jnp.concatenate([rows[:, 128:], jnp.zeros((80, 96), F32)], axis=1)
        lane = lanes((80, 128))
        second = jnp.where(lane < 48, lane_roll(left, 48), lane_roll(right, 48))
        gram[...] = jnp.where(lane < 80, left + second, 0.0)


def gram(dr, qw, z):
    two = pl.BlockSpec((2, 1, NY, S, NZ), lambda x: (0, x, 0, 0, 0))
    one = pl.BlockSpec((1, 1, NY, S, NZ), lambda x: (0, x, 0, 0, 0))
    return pl.pallas_call(
        gram_kernel,
        grid=(NX,),
        in_specs=[two, two, one],
        out_specs=[pl.BlockSpec((NY, 160, NZ), lambda x: (x, 0, 0)), pl.BlockSpec((80, 128), lambda x: (0, 0))],
        out_shape=[jax.ShapeDtypeStruct((NX * NY, 160, NZ), BF16), jax.ShapeDtypeStruct((80, 128), F32)],
        scratch_shapes=[pltpu.VMEM((160, 160), F32)],
        name="gram",
    )(dr, qw, z)


def reduce_all(part):
    for axis in ("gx", "gz"):
        n = lax.axis_size(axis)
        part = part + sum(lax.ppermute(part, axis, [(j, j ^ s) for j in range(n)]) for s in range(1, n))
    n = lax.axis_size("gy")
    spread = jnp.broadcast_to(part[None], (n,) + part.shape)
    return lax.all_to_all(spread, "gy", 0, 0, tiled=True).sum(0)


def rows128(m):
    return jnp.concatenate([m, jnp.zeros((128 - m.shape[0], 128), F32)], axis=0)


def mm(a, b):
    return jnp.dot(a, rows128(b), precision=lax.Precision.HIGHEST, preferred_element_type=F32)


def mm_nt(a, b):
    return lax.dot_general(
        a, rows128(b), (((1,), (1,)), ((), ())), precision=lax.Precision.HIGHEST, preferred_element_type=F32
    )


def eye_at(lane, sub, off):
    return jnp.where(lane == sub + off, 1.0, 0.0).astype(F32)


def spd_inverse(m, lane, sub):
    m = jnp.where(lane < 16, m, eye_at(lane, sub, 16))
    for k in range(S):
        row = m[k : k + 1, :]
        row = row / row[:, k : k + 1]
        m = jnp.where(sub == k, row, m - m[:, k : k + 1] * row)
    return jnp.where(lane < 16, lane_roll(m, 112), 0.0)


def factor_inverse(m, lane, sub):
    m = jnp.where(lane < 16, m, eye_at(lane, sub, 16))
    for k in range(S):
        row = m[k : k + 1, :]
        scale = lax.rsqrt(row[:, k : k + 1])
        row = row * scale
        m = jnp.where(sub == k, row, jnp.where(sub > k, m - (m[:, k : k + 1] * scale) * row, m))
    return jnp.where(lane < 16, lane_roll(m, 112), 0.0)


def step(g, lane, sub):
    gd, gq, gr = g[:16], g[16:32], g[32:48]
    low = lane < 16
    curvature = 0.5 * (lane_roll(gd, 112) + gq)
    inv = spd_inverse(curvature, lane, sub)
    s_t = mm(jnp.where(low, gr, 0.0), inv)
    qq = jnp.where(low, lane_roll(gq, 112), 0.0)
    rq = jnp.where(low, lane_roll(gr, 112), 0.0) - mm(s_t, qq)
    c_t = -mm(rq, inv)
    r_t = eye_at(lane, sub, 32) - lane_roll(s_t, 16)
    f_t = r_t + c_t
    ff = mm_nt(mm(f_t, g), f_t)
    ff = 0.5 * (ff + mm_nt(f_t, mm(f_t, g)))
    inv_factor = factor_inverse(ff, lane, sub)
    return s_t, r_t, mm(inv_factor, f_t)


def algebra_kernel(gram_ref, coef_ref):
    lane = lanes((S, 128))
    sub = lax.broadcasted_iota(jnp.int32, (S, 128), 0)
    g = gram_ref[...] * (1.0 / (64 * 128 * 512))
    lane48 = lanes((48, 128))
    g1 = jnp.where(lane48 < 48, g[:48], 0.0)
    s_t, r_t, d_t = step(g1, lane, sub)
    q_t = (
        lane_roll(jnp.where(lane < 16, d_t, 0.0), 16)
        + lane_roll(jnp.where((lane >= 32) & (lane < 48), d_t, 0.0), 16)
        + lane_roll(jnp.where((lane >= 16) & (lane < 32), d_t, 0.0), 48)
    )
    t = jnp.concatenate([d_t, q_t, r_t], axis=0)
    g2 = mm_nt(mm(t, g), t)
    s2_t, r2_t, d2_t = step(g2, lane, sub)
    final = mm(jnp.concatenate([s2_t, r2_t, d2_t], axis=0), t)
    final = jnp.concatenate([final[:16] + s_t, final[16:]], axis=0)
    hi = final.astype(BF16).astype(F32)
    for i, part in enumerate((hi, final - hi)):
        twice = lane_roll(part, 80)
        coef_ref[48 * i : 48 * i + 48, :128] = jnp.where(lane48 < 80, part, twice).astype(BF16)
        coef_ref[48 * i : 48 * i + 48, 128:] = jnp.where(lane48 < 32, twice, 0.0).astype(BF16)


def algebra(total):
    return pl.pallas_call(
        algebra_kernel,
        in_specs=[VMEM],
        out_specs=VMEM,
        out_shape=jax.ShapeDtypeStruct((96, 256), BF16),
        name="algebra",
    )(total)


def leave_kernel(coef, halves, sol, xo, ro, do):
    left = coef[:, :160]
    flat = [ref.reshape(S * NY, NZ) for ref in (xo, ro, do)]
    inp = sol.reshape(S * NY, NZ)
    for y in range(0, NY, 2):
        pair = jnp.concatenate([halves[y], halves[y + 1]], axis=1)
        res = jnp.dot(left, pair, preferred_element_type=F32)
        res = res[:48] + res[48:]
        for j in range(2):
            v = res[:, j * NZ : (j + 1) * NZ]
            rows = pl.ds(y + j, S, stride=NY)
            flat[0][rows, :] = inp[rows, :] + v[:16]
            flat[1][rows, :] = v[16:32]
            flat[2][rows, :] = v[32:48]


def leave(coef, halves, sol):
    block = pl.BlockSpec((S, 1, NY, NZ), lambda x: (0, x, 0, 0))
    return pl.pallas_call(
        leave_kernel,
        grid=(NX,),
        in_specs=[pl.BlockSpec((96, 256), lambda x: (0, 0)), pl.BlockSpec((NY, 160, NZ), lambda x: (x, 0, 0)), block],
        out_specs=[block] * 3,
        out_shape=[jax.ShapeDtypeStruct((S, NX, NY, NZ), F32)] * 3,
        name="leave",
    )(coef, halves, sol)


def edge_flags():
    vals = []
    for axis in AXES:
        i, n = lax.axis_index(axis), lax.axis_size(axis)
        vals += [i > 0, i < n - 1]
    return jnp.stack(vals).astype(F32)


def body(sol, residual, direction, kappa, cond):
    dr, *faces = enter(direction, residual, cond)
    halos = exchange(faces)
    coef = coefs(edge_flags(), kappa, cond, halos)
    mid, *faces = stencil(dr, halos, coef, 2, 2)
    qw, *faces = stencil(mid, exchange(faces), coef, 2, 1)
    mid, *faces = stencil(qw, exchange(faces), coef, 1, 1)
    (z,) = stencil(mid, exchange(faces), coef, 1, 0)
    halves, part = gram(dr, qw, z)
    return tuple(leave(algebra(reduce_all(part)), halves, sol))


def solution(mesh):
    fields = P(None, *AXES)
    cells = P(*AXES)
    return jax.shard_map(
        body,
        mesh=mesh,
        in_specs=(fields, fields, fields, cells, cells),
        out_specs=(fields, fields, fields),
        check_vma=False,
    )
```

time: 777 us -> 219 us (0.28); the launches traced: 767 us -> 218 us
  blocking collectives: 397 us -> 12 us
  Pallas kernels: 0 us -> 120 us
  local copies, waits for them, and re-layouts: 113 us -> 4.09 us
  matrix products: 67.4 us -> 0 us
  other arithmetic: 65.2 us -> 1.97 us
  starting transfers between devices: 92.2 us -> 56.4 us
    psum x6 -> x0, blocking collectives: 397 us -> none  [the longest x2 143 us: body(): lax.psum((local_gram(direction, image, count), local_gram(direction, resi...]
    pallas_call x0 -> x9, Pallas kernels: none -> 120 us  [the longest x4 65.4 us: stencil(): pl.pallas_call(functools.partial(stencil_kernel, nf, ne), in_specs=[VMEM]...]
    dot_general x16 -> x0, matrix products: 65.6 us -> none  [the longest x8 33.2 us: combine(): jnp.dot(matrix, flat, precision=lax.Precision.HIGHEST).reshape(fields.shape)]
    slice x23 -> x0, local copies, waits for them, and re-layouts: 49.4 us -> none  [the longest x12 32.8 us: with_halo(): lax.slice_in_dim(block, 0, width, axis=dim)]
    add x6 -> x2, other arithmetic: 42.9 us -> 0.81 us  [reduce_all(): part + sum((lax.ppermute(part, axis, [(j, j ^ s) for j in range(n)]) for...]
    ppermute x30, starting transfers between devices: 92.2 us -> 56.4 us  [the longest x12 36.5 us: exchange(): halos.append(lax.ppermute(low, axis, [(j, (j - 1) % n) for j in range(n)]))]
    ppermute x16 -> x0, local copies, waits for them, and re-layouts: 33.9 us -> none  [the longest x8 17 us: with_halo(): lax.ppermute(lax.slice_in_dim(block, 0, width, axis=dim), axis, backward)]
    unnamed x80 -> x48, local copies, waits for them, and re-layouts: 24.8 us -> 3.96 us
  transfers between devices with their start and end apart: 30 -> 30, of which waited for: 14 -> 12; matrix products, arithmetic and copies ran while one was open for 7% -> 0% of each run, Pallas kernels for 0% -> 0%
where the time goes in v1:
time: 219 us; the launch traced here: 218 us
  Pallas kernels  120 us (55%)
  starting transfers between devices  56.4 us (26%)
  waiting for transfers between devices  21.9 us (10%)
  blocking collectives  12 us (5%)
  local copies, waits for them, and re-layouts  4.09 us (2%)
    pallas_call x4, Pallas kernels, stencil(): pl.pallas_call(functools.partial(stencil_kernel, nf, ne), in_specs=[VMEM]...  65.4 us
    ppermute x12, starting transfers between devices, exchange(): halos.append(lax.ppermute(low, axis, [(j, (j - 1) % n) for j in range(n)]))  36.5 us
    pallas_call x1, Pallas kernels, gram(): pl.pallas_call(gram_kernel, grid=(NX,), in_specs=[two, two, one], out_spe...  15.2 us
    pallas_call x1, Pallas kernels, leave(): pl.pallas_call(leave_kernel, grid=(NX,), in_specs=[pl.BlockSpec((96, 256)...  14.1 us
    ppermute x12, starting transfers between devices, exchange(): halos.append(lax.ppermute(high, axis, [(j, (j + 1) % n) for j in range(n)]))  12.9 us
    pallas_call x1, Pallas kernels, enter(): pl.pallas_call(enter_kernel, grid=(NX,), in_specs=[block, block, pl.Block...  12.7 us
    all_to_all x1, blocking collectives, reduce_all(): return lax.all_to_all(spread, 'gy', 0, 0, tiled=True).sum(0)  12 us
    pallas_call x1, Pallas kernels, algebra(): pl.pallas_call(algebra_kernel, in_specs=[VMEM], out_specs=VMEM, out_shape...  9.32 us
  transfers between devices with their start and end apart: 30, of which 12 were waited for; matrix products, arithmetic and copies ran while one was open for 0% of the time, Pallas kernels for 0%

profile of v1, /device:TPU:1, one launch (start us, length us, event | category | flops | bytes accessed | tf_op | source)
XLA Modules:
  0.0 217.6 jit_solution(14032606816380443521)
XLA Ops:
  0.6 12.7 %enter.1 = (f32[2,16,16,16,128]{4,3,2,1,0:T(8,128)}, f32[33,16,128]{2,1,0:T(8,128)}, f32[33,16,128]{2,1,0:T(8,128)}, f32[33,16,128]{2,1,0:T(8,128)}, f32[33,16,1...) custom-call(f32[16,16,16,128]{3,2,1,0:T(8,128)} %d_ref.1, f32[16,16,16,128]{3,2,1,0:T(8,128)} %r_ref.1, ...), custom_call_target="tpu_custom_call" | custom-call | tf_op jit(solution)/shard_map/enter/pallas_call | solution.py:77
  20.9 4.9 %collective-permute-start.4 = (f32[5,16,128]{2,1,0:T(8,128)}, f32[5,16,128]{2,1,0:T(8,128)S(1)}, u32[]{:S(2)}, u32[]{:S(2)}) collective-permute-start(f32[5,16,128]{2,1,0:T(8,128)} %get-tuple-element.38), channel_id=1, source_target_pairs={{0,1},{1,2},{2,3},{3,0},{4,5},{5,6},{6,7},{7,4},{8,9},{9,10},{10,1... | collective-permute-start | bytes 122888 | tf_op jit(solution)/shard_map/ppermute | solution.py:191
  27.9 4.3 %collective-permute-start.5 = (f32[5,16,128]{2,1,0:T(8,128)}, f32[5,16,128]{2,1,0:T(8,128)S(1)}, u32[]{:S(2)}, u32[]{:S(2)}) collective-permute-start(f32[5,16,128]{2,1,0:T(8,128)} %get-tuple-element.39), channel_id=1, source_target_pairs={{0,3},{1,0},{2,1},{3,2},{4,7},{5,4},{6,5},{7,6},{8,11},{9,8},{10,9... | collective-permute-start | bytes 122888 | tf_op jit(solution)/shard_map/ppermute | solution.py:192
  35.2 3.6 %coefs.1.coef = f32[7,16,16,128]{3,2,1,0:T(8,128)} custom-call(f32[6]{0:T(128)} %convert_element_type.3.flag, f32[16,16,128]{2,1,0:T(8,128)} %kappa.1, f32[16,16,128]{2,1,0:T(8,128)} %cond.1, f32[33,16,128]{2,1,0:T(8,128)} %copy-done, f32[33,16,128]{2,1,0:T(8,128)} %copy-done.1, f32[33,16,128]{2,1,0:T(8,128)} %copy-done.2, f32[33,16,128]{2,1,0:T(8,128)} %copy-done.3, ...), custom_call_target="tpu_custom_call" | custom-call | tf_op jit(solution)/shard_map/coefs/pallas_call | solution.py:117
  38.8 28.9 %stencil22.1 = (f32[2,16,16,16,128]{4,3,2,1,0:T(8,128)}, f32[32,16,128]{2,1,0:T(8,128)}, f32[32,16,128]{2,1,0:T(8,128)}, f32[32,16,128]{2,1,0:T(8,128)}, f32[32,...) custom-call(f32[2,16,16,16,128]{4,3,2,1,0:T(8,128)} %get-tuple-element.33.field.dr, ...), custom_call_target="tpu_custom_call" | custom-call | tf_op jit(solution)/shard_map/stencil22/pallas_call | solution.py:176
  67.7 2.7 %collective-permute-start.7 = (f32[32,16,128]{2,1,0:T(8,128)}, f32[32,16,128]{2,1,0:T(8,128)S(1)}, u32[]{:S(2)}, u32[]{:S(2)}) collective-permute-start(f32[32,16,128]{2,1,0:T(8,128)} %get-tuple-element.42), channel_id=1, source_target_pairs={{0,96},{32,0},{64,32},{96,64},{1,97},{33,1},{65,33},{97,65},{2,98}... | collective-permute-start | bytes 786440 | tf_op jit(solution)/shard_map/ppermute | solution.py:192
  70.4 3.6 %collective-permute-start.9 = (f32[32,16,128]{2,1,0:T(8,128)}, f32[32,16,128]{2,1,0:T(8,128)S(1)}, u32[]{:S(2)}, u32[]{:S(2)}) collective-permute-start(f32[32,16,128]{2,1,0:T(8,128)} %get-tuple-element.44), channel_id=1, source_target_pairs={{0,28},{4,0},{8,4},{12,8},{16,12},{20,16},{24,20},{28,24},{1,29},{... | collective-permute-start | bytes 786440 | tf_op jit(solution)/shard_map/ppermute | solution.py:192
  75.5 4.2 %collective-permute-done.10.zl = f32[4,16,128]{2,1,0:T(8,128)S(1)} collective-permute-done((f32[4,16,128]{2,1,0:T(8,128)}, f32[4,16,128]{2,1,0:T(8,128)S(1)}, u32[]{:S(2)}, u32[]{:S(2)}) %collective-permute-start.10) | collective-permute-done | bytes 32800 | tf_op jit(solution)/shard_map/ppermute | solution.py:191
  82.3 3.2 %collective-permute-done.11.zh = f32[4,16,128]{2,1,0:T(8,128)S(1)} collective-permute-done((f32[4,16,128]{2,1,0:T(8,128)}, f32[4,16,128]{2,1,0:T(8,128)S(1)}, u32[]{:S(2)}, u32[]{:S(2)}) %collective-permute-start.11) | collective-permute-done | bytes 32800 | tf_op jit(solution)/shard_map/ppermute | solution.py:192
  86.4 18.5 %stencil21.1 = (f32[2,16,16,16,128]{4,3,2,1,0:T(8,128)}, f32[16,16,128]{2,1,0:T(8,128)}, f32[16,16,128]{2,1,0:T(8,128)}, f32[16,16,128]{2,1,0:T(8,128)}, f32[16,...) custom-call(f32[2,16,16,16,128]{4,3,2,1,0:T(8,128)} %get-tuple-element.40.field, ...), custom_call_target="tpu_custom_call" | custom-call | tf_op jit(solution)/shard_map/stencil21/pallas_call | solution.py:176
  104.9 2.7 %collective-permute-start.13 = (f32[16,16,128]{2,1,0:T(8,128)}, f32[16,16,128]{2,1,0:T(8,128)S(1)}, u32[]{:S(2)}, u32[]{:S(2)}) collective-permute-start(f32[16,16,128]{2,1,0:T(8,128)} %get-tuple-element.49), channel_id=1, source_target_pairs={{0,96},{32,0},{64,32},{96,64},{1,97},{33,1},{65,33},{97,65},{2,98}... | collective-permute-start | bytes 393224 | tf_op jit(solution)/shard_map/ppermute | solution.py:192
  107.6 3.6 %collective-permute-start.15 = (f32[16,16,128]{2,1,0:T(8,128)}, f32[16,16,128]{2,1,0:T(8,128)S(1)}, u32[]{:S(2)}, u32[]{:S(2)}) collective-permute-start(f32[16,16,128]{2,1,0:T(8,128)} %get-tuple-element.51), channel_id=1, source_target_pairs={{0,28},{4,0},{8,4},{12,8},{16,12},{20,16},{24,20},{28,24},{1,29},{... | collective-permute-start | bytes 393224 | tf_op jit(solution)/shard_map/ppermute | solution.py:192
  113.8 3.3 %collective-permute-start.17 = (f32[2,16,128]{2,1,0:T(8,128)}, f32[2,16,128]{2,1,0:T(8,128)S(1)}, u32[]{:S(2)}, u32[]{:S(2)}) collective-permute-start(f32[2,16,128]{2,1,0:T(8,128)} %get-tuple-element.53), channel_id=1, source_target_pairs={{0,3},{1,0},{2,1},{3,2},{4,7},{5,4},{6,5},{7,6},{8,11},{9,8},{10,9... | collective-permute-start | bytes 49160 | tf_op jit(solution)/shard_map/ppermute | solution.py:192
  120.1 10.7 %stencil11.1 = (f32[1,16,16,16,128]{4,3,2,1,0:T(8,128)}, f32[16,16,128]{2,1,0:T(8,128)}, f32[16,16,128]{2,1,0:T(8,128)}, f32[16,16,128]{2,1,0:T(8,128)}, f32[16,...) custom-call(f32[2,16,16,16,128]{4,3,2,1,0:T(8,128)} %get-tuple-element.47.field.qw, ...), custom_call_target="tpu_custom_call" | custom-call | tf_op jit(solution)/shard_map/stencil11/pallas_call | solution.py:176
  130.8 2.7 %collective-permute-start.19 = (f32[16,16,128]{2,1,0:T(8,128)}, f32[16,16,128]{2,1,0:T(8,128)S(1)}, u32[]{:S(2)}, u32[]{:S(2)}) collective-permute-start(f32[16,16,128]{2,1,0:T(8,128)} %get-tuple-element.56), channel_id=1, source_target_pairs={{0,96},{32,0},{64,32},{96,64},{1,97},{33,1},{65,33},{97,65},{2,98}... | collective-permute-start | bytes 393224 | tf_op jit(solution)/shard_map/ppermute | solution.py:192
  133.5 3.9 %collective-permute-start.21 = (f32[16,16,128]{2,1,0:T(8,128)}, f32[16,16,128]{2,1,0:T(8,128)S(1)}, u32[]{:S(2)}, u32[]{:S(2)}) collective-permute-start(f32[16,16,128]{2,1,0:T(8,128)} %get-tuple-element.58), channel_id=1, source_target_pairs={{0,28},{4,0},{8,4},{12,8},{16,12},{20,16},{24,20},{28,24},{1,29},{... | collective-permute-start | bytes 393224 | tf_op jit(solution)/shard_map/ppermute | solution.py:192
  139.9 3.3 %collective-permute-start.23 = (f32[2,16,128]{2,1,0:T(8,128)}, f32[2,16,128]{2,1,0:T(8,128)S(1)}, u32[]{:S(2)}, u32[]{:S(2)}) collective-permute-start(f32[2,16,128]{2,1,0:T(8,128)} %get-tuple-element.60), channel_id=1, source_target_pairs={{0,3},{1,0},{2,1},{3,2},{4,7},{5,4},{6,5},{7,6},{8,11},{9,8},{10,9... | collective-permute-start | bytes 49160 | tf_op jit(solution)/shard_map/ppermute | solution.py:192
  146.1 7.2 %stencil10.1.z = f32[1,16,16,16,128]{4,3,2,1,0:T(8,128)} custom-call(f32[1,16,16,16,128]{4,3,2,1,0:T(8,128)} %get-tuple-element.54.field, f32[16,16,128]{2,1,0:T(8,128)} %copy-done.12, f32[16,16,128]{2,1,0:T(8,128)} %copy-done.14, f32[16,16,128]{2,1,0:T(8,128)} %copy-done.16, f32[16,16,128]{2,1,0:T(8,128)} %copy-done.17, f32[2,16,128]{2,1,0:T(8,128)} %copy-done.21, ...), custom_call_target="tpu_custom_call" | custom-call | tf_op jit(solution)/shard_map/stencil10/pallas_call | solution.py:176
  153.4 15.2 %gram.1 = (bf16[256,160,128]{2,1,0:T(8,128)(2,1)}, f32[80,128]{1,0:T(8,128)}) custom-call(f32[2,16,16,16,128]{4,3,2,1,0:T(8,128)} %get-tuple-element.33.field.dr, f32[2,16,16,16,128]{4,3,2,1,0:T(8,128)} %get-tuple-element.47.field.qw, f32[1,16,16,16,128]{4,3,2,1,0:T(8,128)} %stencil10.1.z), custom_call_target="tpu_custom_call" | custom-call | tf_op jit(solution)/shard_map/gram/pallas_call | solution.py:229
  169.1 2.7 %collective-permute-start.24 = (f32[80,128]{1,0:T(8,128)}, f32[80,128]{1,0:T(8,128)S(1)}, u32[]{:S(2)}, u32[]{:S(2)}) collective-permute-start(f32[80,128]{1,0:T(8,128)} %get-tuple-element.61), channel_id=1, source_target_pairs={{0,32},{32,0},{64,96},{96,64},{1,33},{33,1},{65,97},{97,65},{2,34}... | collective-permute-start | bytes 122888 | tf_op jit(solution)/shard_map/ppermute | solution.py:243
  176.2 3.0 %collective-permute-start.28 = (f32[80,128]{1,0:T(8,128)S(1)}, f32[80,128]{1,0:T(8,128)S(1)}, u32[]{:S(2)}, u32[]{:S(2)}) collective-permute-start(f32[80,128]{1,0:T(8,128)S(1)} %add_add_fusion.1), channel_id=1, source_target_pairs={{0,2},{1,3},{2,0},{3,1},{4,6},{5,7},{6,4},{7,5},{8,10},{9,11},{10,... | collective-permute-start | bytes 122888 | tf_op jit(solution)/shard_map/ppermute | solution.py:243
  181.5 12.0 %all_to_all.5 = f32[8,80,128]{2,1,0:T(8,128)S(1)} all-to-all(f32[8,80,128]{2,1,0:T(8,128)S(1)} %broadcast_in_dim.2), channel_id=1, replica_groups=mesh['gx'=4,'gy'=8,'gz'=4] {'gy'}, dimensions={0} | all-to-all | bytes 655360 | tf_op jit(solution)/shard_map/all_to_all | solution.py:246
  194.1 9.3 %algebra.1.coef = bf16[96,256]{1,0:T(8,128)(2,1)} custom-call(f32[80,128]{1,0:T(8,128)} %reduce_sum.9.gram_ref), custom_call_target="tpu_custom_call" | custom-call | tf_op jit(solution)/shard_map/algebra/pallas_call | solution.py:328
  203.5 14.1 %leave.1 = (f32[16,16,16,128]{3,2,1,0:T(8,128)}, f32[16,16,16,128]{3,2,1,0:T(8,128)}, f32[16,16,16,128]{3,2,1,0:T(8,128)}) custom-call(bf16[96,256]{1,0:T(8,128)(2,1)} %algebra.1.coef, bf16[256,160,128]{2,1,0:T(8,128)(2,1)} %get-tuple-element.62.halves, f32[16,16,16,128]{3,2,1,0:T(8,128)} %sol.1), custom_call_target="tpu_custom_call" | custom-call | tf_op jit(solution)/shard_map/leave/pallas_call | solution.py:355
  (100 shorter events, 36.5 us)
Async XLA Ops:
  13.3 20.3 %collective-permute-start = (f32[33,16,128]{2,1,0:T(8,128)}, f32[33,16,128]{2,1,0:T(8,128)S(1)}, u32[]{:S(2)}, u32[]{:S(2)}) collective-permute-start(f32[33,16,128]{2,1,0:T(8,128)} %get-tuple-element.34), channel_id=1, source_target_pairs={{0,32},{32,64},{64,96},{96,0},{1,33},{33,65},{65,97},{97,1},{2,34}... | collective-permute-start | bytes 811016 | tf_op jit(solution)/shard_map/ppermute | solution.py:191
  15.5 18.1 %collective-permute-start.1 = (f32[33,16,128]{2,1,0:T(8,128)}, f32[33,16,128]{2,1,0:T(8,128)S(1)}, u32[]{:S(2)}, u32[]{:S(2)}) collective-permute-start(f32[33,16,128]{2,1,0:T(8,128)} %get-tuple-element.35), channel_id=1, source_target_pairs={{0,96},{32,0},{64,32},{96,64},{1,97},{33,1},{65,33},{97,65},{2,98}... | collective-permute-start | bytes 811016 | tf_op jit(solution)/shard_map/ppermute | solution.py:192
  17.0 16.6 %collective-permute-start.2 = (f32[33,16,128]{2,1,0:T(8,128)}, f32[33,16,128]{2,1,0:T(8,128)S(1)}, u32[]{:S(2)}, u32[]{:S(2)}) collective-permute-start(f32[33,16,128]{2,1,0:T(8,128)} %get-tuple-element.36), channel_id=1, source_target_pairs={{0,4},{4,8},{8,12},{12,16},{16,20},{20,24},{24,28},{28,0},{1,5},{5... | collective-permute-start | bytes 811016 | tf_op jit(solution)/shard_map/ppermute | solution.py:191
  18.2 15.4 %collective-permute-start.3 = (f32[33,16,128]{2,1,0:T(8,128)}, f32[33,16,128]{2,1,0:T(8,128)S(1)}, u32[]{:S(2)}, u32[]{:S(2)}) collective-permute-start(f32[33,16,128]{2,1,0:T(8,128)} %get-tuple-element.37), channel_id=1, source_target_pairs={{0,28},{4,0},{8,4},{12,8},{16,12},{20,16},{24,20},{28,24},{1,29},{... | collective-permute-start | bytes 811016 | tf_op jit(solution)/shard_map/ppermute | solution.py:192
  20.9 7.0 %collective-permute-start.4 = (f32[5,16,128]{2,1,0:T(8,128)}, f32[5,16,128]{2,1,0:T(8,128)S(1)}, u32[]{:S(2)}, u32[]{:S(2)}) collective-permute-start(f32[5,16,128]{2,1,0:T(8,128)} %get-tuple-element.38), channel_id=1, source_target_pairs={{0,1},{1,2},{2,3},{3,0},{4,5},{5,6},{6,7},{7,4},{8,9},{9,10},{10,1... | collective-permute-start | bytes 122888 | tf_op jit(solution)/shard_map/ppermute | solution.py:191
  27.9 5.7 %collective-permute-start.5 = (f32[5,16,128]{2,1,0:T(8,128)}, f32[5,16,128]{2,1,0:T(8,128)S(1)}, u32[]{:S(2)}, u32[]{:S(2)}) collective-permute-start(f32[5,16,128]{2,1,0:T(8,128)} %get-tuple-element.39), channel_id=1, source_target_pairs={{0,3},{1,0},{2,1},{3,2},{4,7},{5,4},{6,5},{7,6},{8,11},{9,8},{10,9... | collective-permute-start | bytes 122888 | tf_op jit(solution)/shard_map/ppermute | solution.py:192
  67.7 17.7 %collective-permute-start.6 = (f32[32,16,128]{2,1,0:T(8,128)}, f32[32,16,128]{2,1,0:T(8,128)S(1)}, u32[]{:S(2)}, u32[]{:S(2)}) collective-permute-start(f32[32,16,128]{2,1,0:T(8,128)} %get-tuple-element.41), channel_id=1, source_target_pairs={{0,32},{32,64},{64,96},{96,0},{1,33},{33,65},{65,97},{97,1},{2,34}... | collective-permute-start | bytes 786440 | tf_op jit(solution)/shard_map/ppermute | solution.py:191
  67.7 17.7 %collective-permute-start.7 = (f32[32,16,128]{2,1,0:T(8,128)}, f32[32,16,128]{2,1,0:T(8,128)S(1)}, u32[]{:S(2)}, u32[]{:S(2)}) collective-permute-start(f32[32,16,128]{2,1,0:T(8,128)} %get-tuple-element.42), channel_id=1, source_target_pairs={{0,96},{32,0},{64,32},{96,64},{1,97},{33,1},{65,33},{97,65},{2,98}... | collective-permute-start | bytes 786440 | tf_op jit(solution)/shard_map/ppermute | solution.py:192
  70.4 15.1 %collective-permute-start.8 = (f32[32,16,128]{2,1,0:T(8,128)}, f32[32,16,128]{2,1,0:T(8,128)S(1)}, u32[]{:S(2)}, u32[]{:S(2)}) collective-permute-start(f32[32,16,128]{2,1,0:T(8,128)} %get-tuple-element.43), channel_id=1, source_target_pairs={{0,4},{4,8},{8,12},{12,16},{16,20},{20,24},{24,28},{28,0},{1,5},{5... | collective-permute-start | bytes 786440 | tf_op jit(solution)/shard_map/ppermute | solution.py:191
  70.4 15.1 %collective-permute-start.9 = (f32[32,16,128]{2,1,0:T(8,128)}, f32[32,16,128]{2,1,0:T(8,128)S(1)}, u32[]{:S(2)}, u32[]{:S(2)}) collective-permute-start(f32[32,16,128]{2,1,0:T(8,128)} %get-tuple-element.44), channel_id=1, source_target_pairs={{0,28},{4,0},{8,4},{12,8},{16,12},{20,16},{24,20},{28,24},{1,29},{... | collective-permute-start | bytes 786440 | tf_op jit(solution)/shard_map/ppermute | solution.py:192
  74.0 5.8 %collective-permute-start.10 = (f32[4,16,128]{2,1,0:T(8,128)}, f32[4,16,128]{2,1,0:T(8,128)S(1)}, u32[]{:S(2)}, u32[]{:S(2)}) collective-permute-start(f32[4,16,128]{2,1,0:T(8,128)} %get-tuple-element.45), channel_id=1, source_target_pairs={{0,1},{1,2},{2,3},{3,0},{4,5},{5,6},{6,7},{7,4},{8,9},{9,10},{10,1... | collective-permute-start | bytes 98312 | tf_op jit(solution)/shard_map/ppermute | solution.py:191
  79.8 5.7 %collective-permute-start.11 = (f32[4,16,128]{2,1,0:T(8,128)}, f32[4,16,128]{2,1,0:T(8,128)S(1)}, u32[]{:S(2)}, u32[]{:S(2)}) collective-permute-start(f32[4,16,128]{2,1,0:T(8,128)} %get-tuple-element.46), channel_id=1, source_target_pairs={{0,3},{1,0},{2,1},{3,2},{4,7},{5,4},{6,5},{7,6},{8,11},{9,8},{10,9... | collective-permute-start | bytes 98312 | tf_op jit(solution)/shard_map/ppermute | solution.py:192
  104.9 14.4 %collective-permute-start.12 = (f32[16,16,128]{2,1,0:T(8,128)}, f32[16,16,128]{2,1,0:T(8,128)S(1)}, u32[]{:S(2)}, u32[]{:S(2)}) collective-permute-start(f32[16,16,128]{2,1,0:T(8,128)} %get-tuple-element.48), channel_id=1, source_target_pairs={{0,32},{32,64},{64,96},{96,0},{1,33},{33,65},{65,97},{97,1},{2,34}... | collective-permute-start | bytes 393224 | tf_op jit(solution)/shard_map/ppermute | solution.py:191
  104.9 14.4 %collective-permute-start.13 = (f32[16,16,128]{2,1,0:T(8,128)}, f32[16,16,128]{2,1,0:T(8,128)S(1)}, u32[]{:S(2)}, u32[]{:S(2)}) collective-permute-start(f32[16,16,128]{2,1,0:T(8,128)} %get-tuple-element.49), channel_id=1, source_target_pairs={{0,96},{32,0},{64,32},{96,64},{1,97},{33,1},{65,33},{97,65},{2,98}... | collective-permute-start | bytes 393224 | tf_op jit(solution)/shard_map/ppermute | solution.py:192
  107.6 11.7 %collective-permute-start.14 = (f32[16,16,128]{2,1,0:T(8,128)}, f32[16,16,128]{2,1,0:T(8,128)S(1)}, u32[]{:S(2)}, u32[]{:S(2)}) collective-permute-start(f32[16,16,128]{2,1,0:T(8,128)} %get-tuple-element.50), channel_id=1, source_target_pairs={{0,4},{4,8},{8,12},{12,16},{16,20},{20,24},{24,28},{28,0},{1,5},{5... | collective-permute-start | bytes 393224 | tf_op jit(solution)/shard_map/ppermute | solution.py:191
  107.6 11.7 %collective-permute-start.15 = (f32[16,16,128]{2,1,0:T(8,128)}, f32[16,16,128]{2,1,0:T(8,128)S(1)}, u32[]{:S(2)}, u32[]{:S(2)}) collective-permute-start(f32[16,16,128]{2,1,0:T(8,128)} %get-tuple-element.51), channel_id=1, source_target_pairs={{0,28},{4,0},{8,4},{12,8},{16,12},{20,16},{24,20},{28,24},{1,29},{... | collective-permute-start | bytes 393224 | tf_op jit(solution)/shard_map/ppermute | solution.py:192
  130.8 14.5 %collective-permute-start.18 = (f32[16,16,128]{2,1,0:T(8,128)}, f32[16,16,128]{2,1,0:T(8,128)S(1)}, u32[]{:S(2)}, u32[]{:S(2)}) collective-permute-start(f32[16,16,128]{2,1,0:T(8,128)} %get-tuple-element.55), channel_id=1, source_target_pairs={{0,32},{32,64},{64,96},{96,0},{1,33},{33,65},{65,97},{97,1},{2,34}... | collective-permute-start | bytes 393224 | tf_op jit(solution)/shard_map/ppermute | solution.py:191
  130.8 14.5 %collective-permute-start.19 = (f32[16,16,128]{2,1,0:T(8,128)}, f32[16,16,128]{2,1,0:T(8,128)S(1)}, u32[]{:S(2)}, u32[]{:S(2)}) collective-permute-start(f32[16,16,128]{2,1,0:T(8,128)} %get-tuple-element.56), channel_id=1, source_target_pairs={{0,96},{32,0},{64,32},{96,64},{1,97},{33,1},{65,33},{97,65},{2,98}... | collective-permute-start | bytes 393224 | tf_op jit(solution)/shard_map/ppermute | solution.py:192
  133.4 11.9 %collective-permute-start.20 = (f32[16,16,128]{2,1,0:T(8,128)}, f32[16,16,128]{2,1,0:T(8,128)S(1)}, u32[]{:S(2)}, u32[]{:S(2)}) collective-permute-start(f32[16,16,128]{2,1,0:T(8,128)} %get-tuple-element.57), channel_id=1, source_target_pairs={{0,4},{4,8},{8,12},{12,16},{16,20},{20,24},{24,28},{28,0},{1,5},{5... | collective-permute-start | bytes 393224 | tf_op jit(solution)/shard_map/ppermute | solution.py:191
  133.5 11.9 %collective-permute-start.21 = (f32[16,16,128]{2,1,0:T(8,128)}, f32[16,16,128]{2,1,0:T(8,128)S(1)}, u32[]{:S(2)}, u32[]{:S(2)}) collective-permute-start(f32[16,16,128]{2,1,0:T(8,128)} %get-tuple-element.58), channel_id=1, source_target_pairs={{0,28},{4,0},{8,4},{12,8},{16,12},{20,16},{24,20},{28,24},{1,29},{... | collective-permute-start | bytes 393224 | tf_op jit(solution)/shard_map/ppermute | solution.py:192
  168.6 5.8 %collective-permute-start.26 = (f32[80,128]{1,0:T(8,128)}, f32[80,128]{1,0:T(8,128)S(1)}, u32[]{:S(2)}, u32[]{:S(2)}) collective-permute-start(f32[80,128]{1,0:T(8,128)} %get-tuple-element.61), channel_id=1, source_target_pairs={{0,96},{32,64},{64,32},{96,0},{1,97},{33,65},{65,33},{97,1},{2,98}... | collective-permute-start | bytes 122888 | tf_op jit(solution)/shard_map/ppermute | solution.py:243
  168.6 5.8 %collective-permute-start.25 = (f32[80,128]{1,0:T(8,128)}, f32[80,128]{1,0:T(8,128)S(1)}, u32[]{:S(2)}, u32[]{:S(2)}) collective-permute-start(f32[80,128]{1,0:T(8,128)} %get-tuple-element.61), channel_id=1, source_target_pairs={{0,64},{32,96},{64,0},{96,32},{1,65},{33,97},{65,1},{97,33},{2,66}... | collective-permute-start | bytes 122888 | tf_op jit(solution)/shard_map/ppermute | solution.py:243
  169.1 5.7 %collective-permute-start.24 = (f32[80,128]{1,0:T(8,128)}, f32[80,128]{1,0:T(8,128)S(1)}, u32[]{:S(2)}, u32[]{:S(2)}) collective-permute-start(f32[80,128]{1,0:T(8,128)} %get-tuple-element.61), channel_id=1, source_target_pairs={{0,32},{32,0},{64,96},{96,64},{1,33},{33,1},{65,97},{97,65},{2,34}... | collective-permute-start | bytes 122888 | tf_op jit(solution)/shard_map/ppermute | solution.py:243
  175.6 5.6 %collective-permute-start.29 = (f32[80,128]{1,0:T(8,128)S(1)}, f32[80,128]{1,0:T(8,128)S(1)}, u32[]{:S(2)}, u32[]{:S(2)}) collective-permute-start(f32[80,128]{1,0:T(8,128)S(1)} %add_add_fusion.1), channel_id=1, source_target_pairs={{0,3},{1,2},{2,1},{3,0},{4,7},{5,6},{6,5},{7,4},{8,11},{9,10},{10,... | collective-permute-start | bytes 122888 | tf_op jit(solution)/shard_map/ppermute | solution.py:243
  (30 other events, 60.6 us)

commit v2 on v1

--- a/solution.py
+++ b/solution.py
@@ -12,7 +12,10 @@
 NX, NY, NZ = 16, 16, 128
 F32, BF16 = jnp.float32, jnp.bfloat16
 VMEM = pl.BlockSpec(memory_space=pltpu.VMEM)
-PARAMS = pltpu.CompilerParams(vmem_limit_bytes=56 << 20)
+
+
+def grant(mib):
+    return pltpu.CompilerParams(vmem_limit_bytes=mib << 20)
 
 
 def lanes(shape):
@@ -23,36 +26,36 @@
     return pltpu.roll(v, shift, v.ndim - 1)
 
 
+def pack_z(acc, v, y, lane):
+    return jnp.where((lane == 2 * y) | (lane == 2 * y + 1), lane_roll(v, 2 * y + 1), acc)
+
+
 def put_z_face(ref, row, acc, off, lane):
     moved = lane_roll(acc, off)
-    ref[row] = jnp.where((lane >= off) & (lane < off + NY), moved, ref[row])
-
-
-def enter_kernel(d_ref, r_ref, c_ref, out_ref, xl, xh, yl, yh, zl, zh):
+    ref[row] = jnp.where((lane >= off) & (lane < off + 2 * NY), moved, ref[row])
+
+
+def enter_kernel(d_ref, r_ref, c_ref, out_ref, xl, xh, yl, yh, zf):
     x = pl.program_id(0)
     lane = lanes((S, NZ))
-    off = lax.rem(x, 8) * NY
+    off = lax.rem(x, 4) * 32
     for f, ref in enumerate((d_ref, r_ref)):
         flat = ref.reshape(S * NY, NZ)
-        accl = jnp.zeros((S, NZ), F32)
-        acch = jnp.zeros((S, NZ), F32)
+        acc = jnp.zeros((S, NZ), F32)
         for y in range(NY):
             v = flat[pl.ds(y, S, stride=NY), :]
             out_ref[f, 0, y] = v
-            accl = jnp.where(lane == y, lane_roll(v, y) if y else v, accl)
-            acch = jnp.where(lane == y, lane_roll(v, y + 1), acch)
+            acc = pack_z(acc, v, y, lane)
             if y == 0:
                 yl[f * NX + x] = v
             if y == NY - 1:
                 yh[f * NX + x] = v
-        put_z_face(zl, f * 2 + x // 8, accl, off, lane)
-        put_z_face(zh, f * 2 + x // 8, acch, off, lane)
+        put_z_face(zf, f * 4 + x // 4, acc, off, lane)
 
     cond = c_ref[0]
     yl[2 * NX, pl.ds(x, 1), :] = cond[0:1]
     yh[2 * NX, pl.ds(x, 1), :] = cond[NY - 1 : NY]
-    zl[4] = jnp.where(lane == x, lane_roll(cond, x), zl[4])
-    zh[4] = jnp.where(lane == x, lane_roll(cond, x + 1), zh[4])
+    zf[8] = jnp.where((lane == 2 * x) | (lane == 2 * x + 1), lane_roll(cond, 2 * x + 1), zf[8])
 
     @pl.when(x == 0)
     def _():
@@ -73,13 +76,14 @@
     block = pl.BlockSpec((S, 1, NY, NZ), lambda x: (0, x, 0, 0))
     whole = lambda n: pl.BlockSpec((n, S, NZ), lambda x: (0, 0, 0))
     shape = lambda n: jax.ShapeDtypeStruct((n, S, NZ), F32)
-    rows = (33, 33, 33, 33, 5, 5)
+    rows = (33, 33, 33, 33, 9)
     return pl.pallas_call(
         enter_kernel,
         grid=(NX,),
         in_specs=[block, block, pl.BlockSpec((1, NY, NZ), lambda x: (x, 0, 0))],
         out_specs=[pl.BlockSpec((2, 1, NY, S, NZ), lambda x: (0, x, 0, 0, 0))] + [whole(n) for n in rows],
         out_shape=[jax.ShapeDtypeStruct((2, NX, NY, S, NZ), F32)] + [shape(n) for n in rows],
+        compiler_params=grant(4),
         name="enter",
     )(direction, residual, conductance)
 
@@ -96,8 +100,8 @@
         yhi = yh[2 * NX, pl.ds(x, 1), :] * flag[3]
         ym = jnp.where(sub == 0, ylo, pltpu.roll(c, 1, 0))
         yp = jnp.where(sub == NY - 1, yhi, pltpu.roll(c, NY - 1, 0))
-        zlo = lane_roll(zl[4], lax.rem(NZ - x, NZ)) * flag[4]
-        zhi = lane_roll(zh[4], NZ - 1 - x) * flag[5]
+        zlo = lane_roll(zl[8], lax.rem(NZ - 2 * x, NZ)) * flag[4]
+        zhi = lane_roll(zh[8], NZ - 2 - 2 * x) * flag[5]
         zm = jnp.where(lane == 0, zlo, lane_roll(c, 1))
         zp = jnp.where(lane == NZ - 1, zhi, lane_roll(c, NZ - 1))
         g = [0.5 * (c + n) for n in (prev, nxt, ym, yp, zm, zp)]
@@ -119,7 +123,7 @@
         in_specs=[pl.BlockSpec(memory_space=pltpu.SMEM)] + [VMEM] * 8,
         out_specs=VMEM,
         out_shape=jax.ShapeDtypeStruct((7, NX, NY, NZ), F32),
-        compiler_params=PARAMS,
+        compiler_params=grant(4),
         name="coefs",
     )(flags, kappa, cond, *halos)
 
@@ -127,32 +131,31 @@
 def stencil_kernel(nf, ne, field, xl, xh, yl, yh, zl, zh, coef, out, *faces):
     lane = lanes((S, NZ))
     first, last = lane == 0, lane == NZ - 1
+    even = lax.rem(lane, 2) == 0
     if ne:
-        oxl, oxh, oyl, oyh, ozl, ozh = faces
+        oxl, oxh, oyl, oyh, ozf = faces
 
     def per_x(x, edge):
-        off = lax.rem(x, 8) * NY
-        back = lax.rem(NZ - off, NZ)
-        half = x // 8
-        zlo = [lane_roll(zl[f * 2 + half], back) for f in range(nf)]
-        zhi = [lane_roll(zh[f * 2 + half], back) for f in range(nf)]
-        accl = [jnp.zeros((S, NZ), F32) for _ in range(ne)]
-        acch = [jnp.zeros((S, NZ), F32) for _ in range(ne)]
-        for y in range(NY):
-            k = [jnp.broadcast_to(coef[i, x, y : y + 1, :], (S, NZ)) for i in range(7)]
-            for f in range(nf):
+        off = lax.rem(x, 4) * 32
+        quarter = x // 4
+        for f in range(nf):
+            beyond = jnp.where(even, lane_roll(zl[f * 4 + quarter], 2), zh[f * 4 + quarter])
+            beyond = lane_roll(beyond, lax.rem(NZ - off, NZ))
+            acc = jnp.zeros((S, NZ), F32)
+            for y in range(NY):
+                k = [jnp.broadcast_to(coef[i, x, y : y + 1, :], (S, NZ)) for i in range(7)]
                 c = field[f, x, y]
                 xm = xl[f * NY + y] if edge == "lo" else field[f, x - 1, y]
                 xp = xh[f * NY + y] if edge == "hi" else field[f, x + 1, y]
                 ym = field[f, x, y - 1] if y else yl[f * NX + x]
                 yp = field[f, x, y + 1] if y < NY - 1 else yh[f * NX + x]
-                zm = jnp.where(first, lane_roll(zlo[f], (NZ - y) % NZ) if y else zlo[f], lane_roll(c, 1))
-                zp = jnp.where(last, lane_roll(zhi[f], NZ - 1 - y), lane_roll(c, NZ - 1))
+                ends = lane_roll(beyond, NZ - 2 - 2 * y)
+                zm = jnp.where(first, ends, lane_roll(c, 1))
+                zp = jnp.where(last, ends, lane_roll(c, NZ - 1))
                 o = ((k[0] * c - k[1] * xm) - (k[2] * xp + k[3] * ym)) - ((k[4] * yp + k[5] * zm) + k[6] * zp)
                 out[f, x, y] = o
                 if f < ne:
-                    accl[f] = jnp.where(lane == y, lane_roll(o, y) if y else o, accl[f])
-                    acch[f] = jnp.where(lane == y, lane_roll(o, y + 1), acch[f])
+                    acc = pack_z(acc, o, y, lane)
                     if edge == "lo":
                         oxl[f * NY + y] = o
                     if edge == "hi":
@@ -161,9 +164,8 @@
                         oyl[f * NX + x] = o
                     if y == NY - 1:
                         oyh[f * NX + x] = o
-        for f in range(ne):
-            put_z_face(ozl, f * 2 + half, accl[f], off, lane)
-            put_z_face(ozh, f * 2 + half, acch[f], off, lane)
+            if f < ne:
+                put_z_face(ozf, f * 4 + quarter, acc, off, lane)
 
     per_x(jnp.int32(0), "lo")
     lax.fori_loop(1, NX - 1, lambda x, c: (per_x(x, ""), c)[1], 0)
@@ -172,22 +174,22 @@
 
 def stencil(field, halos, coef, nf, ne):
     shape = lambda n: jax.ShapeDtypeStruct((n, S, NZ), F32)
-    faces = [shape(n) for n in (16 * ne, 16 * ne, 16 * ne, 16 * ne, 2 * ne, 2 * ne)] if ne else []
+    faces = [shape(n) for n in (16 * ne, 16 * ne, 16 * ne, 16 * ne, 4 * ne)] if ne else []
     return pl.pallas_call(
         functools.partial(stencil_kernel, nf, ne),
         in_specs=[VMEM] * 8,
         out_specs=[VMEM] * (1 + len(faces)),
         out_shape=[jax.ShapeDtypeStruct((nf, NX, NY, S, NZ), F32)] + faces,
-        compiler_params=PARAMS,
+        compiler_params=grant(6 * nf + 3),
         name=f"stencil{nf}{ne}",
     )(field, *halos, coef)
 
 
 def exchange(faces):
+    xl, xh, yl, yh, zf = faces
     halos = []
-    for i, axis in enumerate(AXES):
+    for axis, low, high in (("gx", xl, xh), ("gy", yl, yh), ("gz", zf, zf)):
         n = lax.axis_size(axis)
-        low, high = faces[2 * i], faces[2 * i + 1]
         halos.append(lax.ppermute(high, axis, [(j, (j + 1) % n) for j in range(n)]))
         halos.append(lax.ppermute(low, axis, [(j, (j - 1) % n) for j in range(n)]))
     return halos
@@ -233,6 +235,7 @@
         out_specs=[pl.BlockSpec((NY, 160, NZ), lambda x: (x, 0, 0)), pl.BlockSpec((80, 128), lambda x: (0, 0))],
         out_shape=[jax.ShapeDtypeStruct((NX * NY, 160, NZ), BF16), jax.ShapeDtypeStruct((80, 128), F32)],
         scratch_shapes=[pltpu.VMEM((160, 160), F32)],
+        compiler_params=grant(5),
         name="gram",
     )(dr, qw, z)
 
@@ -330,6 +333,7 @@
         in_specs=[VMEM],
         out_specs=VMEM,
         out_shape=jax.ShapeDtypeStruct((96, 256), BF16),
+        compiler_params=grant(2),
         name="algebra",
     )(total)
 
@@ -358,6 +362,7 @@
         in_specs=[pl.BlockSpec((96, 256), lambda x: (0, 0)), pl.BlockSpec((NY, 160, NZ), lambda x: (x, 0, 0)), block],
         out_specs=[block] * 3,
         out_shape=[jax.ShapeDtypeStruct((S, NX, NY, NZ), F32)] * 3,
+        compiler_params=grant(8),
         name="leave",
     )(coef, halves, sol)
 

time: 219 us -> 162 us (0.74)
  Pallas kernels: 120 us -> 55.8 us
  local copies, waits for them, and re-layouts: 4.09 us -> 16.4 us
  waiting for transfers between devices: 21.9 us -> 33 us
  starting transfers between devices: 56.4 us -> 45.7 us
    pallas_call x4, Pallas kernels: 65.4 us -> 26 us  [stencil(): pl.pallas_call(functools.partial(stencil_kernel, nf, ne), in_specs=[VMEM]...]
    ppermute x12, waiting for transfers between devices: 8.32 us -> 23.1 us  [exchange(): halos.append(lax.ppermute(low, axis, [(j, (j - 1) % n) for j in range(n)]))]
    unnamed x48 -> x22, local copies, waits for them, and re-layouts: 3.96 us -> 16.2 us
    ppermute x12, starting transfers between devices: 12.9 us -> 3.44 us  [exchange(): halos.append(lax.ppermute(high, axis, [(j, (j + 1) % n) for j in range(n)]))]
    pallas_call x1, Pallas kernels: 15.2 us -> 6.85 us  [gram(): pl.pallas_call(gram_kernel, grid=(NX,), in_specs=[two, two, one], out_spe...]
    pallas_call x1, Pallas kernels: 12.7 us -> 4.4 us  [enter(): pl.pallas_call(enter_kernel, grid=(NX,), in_specs=[block, block, pl.Block...]
    pallas_call x1, Pallas kernels: 14.1 us -> 8.71 us  [leave(): pl.pallas_call(leave_kernel, grid=(NX,), in_specs=[pl.BlockSpec((96, 256)...]
    ppermute x12, starting transfers between devices: 36.5 us -> 32.6 us  [exchange(): halos.append(lax.ppermute(low, axis, [(j, (j - 1) % n) for j in range(n)]))]
where the time goes in v2:
time: 162 us
  Pallas kernels  55.8 us (34%)
  starting transfers between devices  45.7 us (28%)
  waiting for transfers between devices  33 us (20%)
  local copies, waits for them, and re-layouts  16.4 us (10%)
  blocking collectives  10.2 us (6%)
    ppermute x12, starting transfers between devices, exchange(): halos.append(lax.ppermute(low, axis, [(j, (j - 1) % n) for j in range(n)]))  32.6 us
    pallas_call x4, Pallas kernels, stencil(): pl.pallas_call(functools.partial(stencil_kernel, nf, ne), in_specs=[VMEM]...  26 us
    ppermute x12, waiting for transfers between devices, exchange(): halos.append(lax.ppermute(low, axis, [(j, (j - 1) % n) for j in range(n)]))  23.1 us
    unnamed x22, local copies, waits for them, and re-layouts  16.2 us
    all_to_all x1, blocking collectives, reduce_all(): return lax.all_to_all(spread, 'gy', 0, 0, tiled=True).sum(0)  10.2 us
    ppermute x6, starting transfers between devices, reduce_all(): lax.ppermute(part, axis, [(j, j ^ s) for j in range(n)])  9.73 us
    pallas_call x1, Pallas kernels, leave(): pl.pallas_call(leave_kernel, grid=(NX,), in_specs=[pl.BlockSpec((96, 256)...  8.71 us
    pallas_call x1, Pallas kernels, algebra(): pl.pallas_call(algebra_kernel, in_specs=[VMEM], out_specs=VMEM, out_shape...  7.93 us
  transfers between devices with their start and end apart: 30, of which 12 were waited for; matrix products, arithmetic and copies ran while one was open for 0% of the time, Pallas kernels for 0%

profile of v2, /device:TPU:1, one launch (start us, length us, event | category | flops | bytes accessed | tf_op | source)
XLA Modules:
  0.0 162.0 jit_solution(225416250350612181)
XLA Ops:
  4.7 4.4 %enter.1 = (f32[2,16,16,16,128]{4,3,2,1,0:T(8,128)S(1)}, f32[33,16,128]{2,1,0:T(8,128)S(1)}, f32[33,16,128]{2,1,0:T(8,128)S(1)}, f32[33,16,128]{2,1,0:T(8,128)S(...) custom-call(f32[16,16,16,128]{3,2,1,0:T(8,128)S(1)} %copy-done.5, f32[16,16,16,128]{3,2,1,0:T(8,128)S(1)} %copy-done.6, ...), custom_call_target="tpu_custom_call" | custom-call | tf_op jit(solution)/shard_map/enter/pallas_call | solution.py:80
  20.0 9.3 %collective-permute-done.5.zh = f32[9,16,128]{2,1,0:T(8,128)S(1)} collective-permute-done((f32[9,16,128]{2,1,0:T(8,128)S(1)}, f32[9,16,128]{2,1,0:T(8,128)S(1)}, u32[]{:S(2)}, u32[]{:S(2)}) %collective-permute-start.5) | collective-permute-done | bytes 73760 | tf_op jit(solution)/shard_map/ppermute | solution.py:194
  34.8 8.7 %stencil22.1 = (f32[2,16,16,16,128]{4,3,2,1,0:T(8,128)S(1)}, f32[32,16,128]{2,1,0:T(8,128)S(1)}, f32[32,16,128]{2,1,0:T(8,128)S(1)}, f32[32,16,128]{2,1,0:T(8,12...) custom-call(f32[2,16,16,16,128]{4,3,2,1,0:T(8,128)S(1)} %copy-done.1, ...), custom_call_target="tpu_custom_call" | custom-call | tf_op jit(solution)/shard_map/stencil22/pallas_call | solution.py:178
  46.2 3.6 %collective-permute-start.9 = (f32[32,16,128]{2,1,0:T(8,128)S(1)}, f32[32,16,128]{2,1,0:T(8,128)S(1)}, u32[]{:S(2)}, u32[]{:S(2)}) collective-permute-start(f32[32,16,128]{2,1,0:T(8,128)S(1)} %get-tuple-element.39), channel_id=1, source_target_pairs={{0,28},{4,0},{8,4},{12,8},{16,12},{20,16},{24,20},{28,24},{1,29},{... | collective-permute-start | bytes 786440 | tf_op jit(solution)/shard_map/ppermute | solution.py:194
  51.6 6.3 %collective-permute-done.11.zh = f32[8,16,128]{2,1,0:T(8,128)S(1)} collective-permute-done((f32[8,16,128]{2,1,0:T(8,128)S(1)}, f32[8,16,128]{2,1,0:T(8,128)S(1)}, u32[]{:S(2)}, u32[]{:S(2)}) %collective-permute-start.11) | collective-permute-done | bytes 65568 | tf_op jit(solution)/shard_map/ppermute | solution.py:194
  59.2 7.2 %stencil21.1 = (f32[2,16,16,16,128]{4,3,2,1,0:T(8,128)S(1)}, f32[16,16,128]{2,1,0:T(8,128)S(1)}, f32[16,16,128]{2,1,0:T(8,128)S(1)}, f32[16,16,128]{2,1,0:T(8,12...) custom-call(f32[2,16,16,16,128]{4,3,2,1,0:T(8,128)S(1)} %get-tuple-element.35.field, ...), custom_call_target="tpu_custom_call" | custom-call | tf_op jit(solution)/shard_map/stencil21/pallas_call | solution.py:178
  69.1 3.6 %collective-permute-start.15 = (f32[16,16,128]{2,1,0:T(8,128)S(1)}, f32[16,16,128]{2,1,0:T(8,128)S(1)}, u32[]{:S(2)}, u32[]{:S(2)}) collective-permute-start(f32[16,16,128]{2,1,0:T(8,128)S(1)} %get-tuple-element.45), channel_id=1, source_target_pairs={{0,28},{4,0},{8,4},{12,8},{16,12},{20,16},{24,20},{28,24},{1,29},{... | collective-permute-start | bytes 393224 | tf_op jit(solution)/shard_map/ppermute | solution.py:194
  72.7 3.3 %collective-permute-start.17 = (f32[4,16,128]{2,1,0:T(8,128)S(1)}, f32[4,16,128]{2,1,0:T(8,128)S(1)}, u32[]{:S(2)}, u32[]{:S(2)}) collective-permute-start(f32[4,16,128]{2,1,0:T(8,128)S(1)} %get-tuple-element.46), channel_id=1, source_target_pairs={{0,3},{1,0},{2,1},{3,2},{4,7},{5,4},{6,5},{7,6},{8,11},{9,8},{10,9... | collective-permute-start | bytes 98312 | tf_op jit(solution)/shard_map/ppermute | solution.py:194
  76.0 4.3 %collective-permute-done.17.zh = f32[4,16,128]{2,1,0:T(8,128)S(1)} collective-permute-done((f32[4,16,128]{2,1,0:T(8,128)S(1)}, f32[4,16,128]{2,1,0:T(8,128)S(1)}, u32[]{:S(2)}, u32[]{:S(2)}) %collective-permute-start.17) | collective-permute-done | bytes 32800 | tf_op jit(solution)/shard_map/ppermute | solution.py:194
  81.5 6.1 %stencil11.1 = (f32[1,16,16,16,128]{4,3,2,1,0:T(8,128)S(1)}, f32[16,16,128]{2,1,0:T(8,128)S(1)}, f32[16,16,128]{2,1,0:T(8,128)S(1)}, f32[16,16,128]{2,1,0:T(8,12...) custom-call(f32[2,16,16,16,128]{4,3,2,1,0:T(8,128)S(1)} %get-tuple-element.41.field.qw, ...), custom_call_target="tpu_custom_call" | custom-call | tf_op jit(solution)/shard_map/stencil11/pallas_call | solution.py:178
  87.6 2.7 %collective-permute-start.19 = (f32[16,16,128]{2,1,0:T(8,128)S(1)}, f32[16,16,128]{2,1,0:T(8,128)S(1)}, u32[]{:S(2)}, u32[]{:S(2)}) collective-permute-start(f32[16,16,128]{2,1,0:T(8,128)S(1)} %get-tuple-element.49), channel_id=1, source_target_pairs={{0,96},{32,0},{64,32},{96,64},{1,97},{33,1},{65,33},{97,65},{2,98}... | collective-permute-start | bytes 393224 | tf_op jit(solution)/shard_map/ppermute | solution.py:194
  90.3 3.6 %collective-permute-start.21 = (f32[16,16,128]{2,1,0:T(8,128)S(1)}, f32[16,16,128]{2,1,0:T(8,128)S(1)}, u32[]{:S(2)}, u32[]{:S(2)}) collective-permute-start(f32[16,16,128]{2,1,0:T(8,128)S(1)} %get-tuple-element.51), channel_id=1, source_target_pairs={{0,28},{4,0},{8,4},{12,8},{16,12},{20,16},{24,20},{28,24},{1,29},{... | collective-permute-start | bytes 393224 | tf_op jit(solution)/shard_map/ppermute | solution.py:194
  93.9 3.3 %collective-permute-start.23 = (f32[4,16,128]{2,1,0:T(8,128)S(1)}, f32[4,16,128]{2,1,0:T(8,128)S(1)}, u32[]{:S(2)}, u32[]{:S(2)}) collective-permute-start(f32[4,16,128]{2,1,0:T(8,128)S(1)} %get-tuple-element.52), channel_id=1, source_target_pairs={{0,3},{1,0},{2,1},{3,2},{4,7},{5,4},{6,5},{7,6},{8,11},{9,8},{10,9... | collective-permute-start | bytes 98312 | tf_op jit(solution)/shard_map/ppermute | solution.py:194
  97.2 3.2 %collective-permute-done.23.zh = f32[4,16,128]{2,1,0:T(8,128)S(1)} collective-permute-done((f32[4,16,128]{2,1,0:T(8,128)S(1)}, f32[4,16,128]{2,1,0:T(8,128)S(1)}, u32[]{:S(2)}, u32[]{:S(2)}) %collective-permute-start.23) | collective-permute-done | bytes 32800 | tf_op jit(solution)/shard_map/ppermute | solution.py:194
  101.6 4.0 %stencil10.1.z = f32[1,16,16,16,128]{4,3,2,1,0:T(8,128)S(1)} custom-call(f32[1,16,16,16,128]{4,3,2,1,0:T(8,128)S(1)} %get-tuple-element.47.field, f32[16,16,128]{2,1,0:T(8,128)S(1)} %collective-permute-done.18.xl, f32[16,16,128]{2,1,0:T(8,128)S(1)} %collective-permute-done.19.xh, f32[16,16,128]{2,1,0:T(8,128)S(1)} %collective-permute-done.20.yl, ...), custom_call_target="tpu_custom_call" | custom-call | tf_op jit(solution)/shard_map/stencil10/pallas_call | solution.py:178
  105.6 6.8 %gram.1 = (bf16[256,160,128]{2,1,0:T(8,128)(2,1)S(1)}, f32[80,128]{1,0:T(8,128)S(1)}) custom-call(f32[2,16,16,16,128]{4,3,2,1,0:T(8,128)S(1)} %copy-done.2, f32[2,16,16,16,128]{4,3,2,1,0:T(8,128)S(1)} %get-tuple-element.41.field.qw, f32[1,16,16,16,128]{4,3,2,1,0:T(8,128)S(1)} %stencil10.1.z), custom_call_target="tpu_custom_call" | custom-call | tf_op jit(solution)/shard_map/gram/pallas_call | solution.py:231
  112.5 4.0 %copy-done.3 = bf16[256,160,128]{2,1,0:T(8,128)(2,1)} copy-done((bf16[256,160,128]{2,1,0:T(8,128)(2,1)}, bf16[256,160,128]{2,1,0:T(8,128)(2,1)S(1)}, u32[]{:S(2)}) %copy-start.3) | copy-done | bytes 10485784
  116.9 2.9 %collective-permute-start.24 = (f32[80,128]{1,0:T(8,128)S(1)}, f32[80,128]{1,0:T(8,128)S(1)}, u32[]{:S(2)}, u32[]{:S(2)}) collective-permute-start(f32[80,128]{1,0:T(8,128)S(1)} %get-tuple-element.53), channel_id=1, source_target_pairs={{0,32},{32,0},{64,96},{96,64},{1,33},{33,1},{65,97},{97,65},{2,34}... | collective-permute-start | bytes 122888 | tf_op jit(solution)/shard_map/ppermute | solution.py:246
  121.6 5.2 %collective-permute-start.29 = (f32[80,128]{1,0:T(8,128)S(1)}, f32[80,128]{1,0:T(8,128)S(1)}, u32[]{:S(2)}, u32[]{:S(2)}) collective-permute-start(f32[80,128]{1,0:T(8,128)S(1)} %add_add_fusion.1), channel_id=1, source_target_pairs={{0,3},{1,2},{2,1},{3,0},{4,7},{5,6},{6,5},{7,4},{8,11},{9,10},{10,... | collective-permute-start | bytes 122888 | tf_op jit(solution)/shard_map/ppermute | solution.py:246
  128.4 2.7 %collective-permute-done.28 = f32[80,128]{1,0:T(8,128)S(1)} collective-permute-done((f32[80,128]{1,0:T(8,128)S(1)}, f32[80,128]{1,0:T(8,128)S(1)}, u32[]{:S(2)}, u32[]{:S(2)}) %collective-permute-start.28) | collective-permute-done | bytes 40992 | tf_op jit(solution)/shard_map/ppermute | solution.py:246
  131.1 10.2 %all_to_all.5 = f32[8,80,128]{2,1,0:T(8,128)S(1)} all-to-all(f32[8,80,128]{2,1,0:T(8,128)S(1)} %broadcast_in_dim.2), channel_id=1, replica_groups=mesh['gx'=4,'gy'=8,'gz'=4] {'gy'}, dimensions={0} | all-to-all | bytes 655360 | tf_op jit(solution)/shard_map/all_to_all | solution.py:249
  141.4 7.9 %algebra.1.coef = bf16[96,256]{1,0:T(8,128)(2,1)S(1)} custom-call(f32[80,128]{1,0:T(8,128)S(1)} %reduce_sum.9.gram_ref), custom_call_target="tpu_custom_call" | custom-call | tf_op jit(solution)/shard_map/algebra/pallas_call | solution.py:331
  149.4 4.0 %copy-done.4 = bf16[256,160,128]{2,1,0:T(8,128)(2,1)S(1)} copy-done((bf16[256,160,128]{2,1,0:T(8,128)(2,1)S(1)}, bf16[256,160,128]{2,1,0:T(8,128)(2,1)}, u32[]{:S(2)}) %copy-start.4) | copy-done | bytes 10485784
  153.3 8.7 %leave.1 = (f32[16,16,16,128]{3,2,1,0:T(8,128)}, f32[16,16,16,128]{3,2,1,0:T(8,128)}, f32[16,16,16,128]{3,2,1,0:T(8,128)}) custom-call(bf16[96,256]{1,0:T(8,128)(2,1)S(1)} %algebra.1.coef, bf16[256,160,128]{2,1,0:T(8,128)(2,1)S(1)} %copy-done.4, f32[16,16,16,128]{3,2,1,0:T(8,128)S(1)} %copy-done.7), custom_call_target="tpu_custom_call" | custom-call | tf_op jit(solution)/shard_map/leave/pallas_call | solution.py:359
  (74 shorter events, 35.4 us)
Async XLA Ops:
  11.1 19.6 %collective-permute-start = (f32[33,16,128]{2,1,0:T(8,128)S(1)}, f32[33,16,128]{2,1,0:T(8,128)S(1)}, u32[]{:S(2)}, u32[]{:S(2)}) collective-permute-start(f32[33,16,128]{2,1,0:T(8,128)S(1)} %get-tuple-element.30), channel_id=1, source_target_pairs={{0,32},{32,64},{64,96},{96,0},{1,33},{33,65},{65,97},{97,1},{2,34}... | collective-permute-start | bytes 811016 | tf_op jit(solution)/shard_map/ppermute | solution.py:193
  13.2 17.4 %collective-permute-start.1 = (f32[33,16,128]{2,1,0:T(8,128)S(1)}, f32[33,16,128]{2,1,0:T(8,128)S(1)}, u32[]{:S(2)}, u32[]{:S(2)}) collective-permute-start(f32[33,16,128]{2,1,0:T(8,128)S(1)} %get-tuple-element.31), channel_id=1, source_target_pairs={{0,96},{32,0},{64,32},{96,64},{1,97},{33,1},{65,33},{97,65},{2,98}... | collective-permute-start | bytes 811016 | tf_op jit(solution)/shard_map/ppermute | solution.py:194
  14.7 16.0 %collective-permute-start.2 = (f32[33,16,128]{2,1,0:T(8,128)S(1)}, f32[33,16,128]{2,1,0:T(8,128)S(1)}, u32[]{:S(2)}, u32[]{:S(2)}) collective-permute-start(f32[33,16,128]{2,1,0:T(8,128)S(1)} %get-tuple-element.32), channel_id=1, source_target_pairs={{0,4},{4,8},{8,12},{12,16},{16,20},{20,24},{24,28},{28,0},{1,5},{5... | collective-permute-start | bytes 811016 | tf_op jit(solution)/shard_map/ppermute | solution.py:193
  15.9 14.8 %collective-permute-start.3 = (f32[33,16,128]{2,1,0:T(8,128)S(1)}, f32[33,16,128]{2,1,0:T(8,128)S(1)}, u32[]{:S(2)}, u32[]{:S(2)}) collective-permute-start(f32[33,16,128]{2,1,0:T(8,128)S(1)} %get-tuple-element.33), channel_id=1, source_target_pairs={{0,28},{4,0},{8,4},{12,8},{16,12},{20,16},{24,20},{28,24},{1,29},{... | collective-permute-start | bytes 811016 | tf_op jit(solution)/shard_map/ppermute | solution.py:194
  18.5 10.7 %collective-permute-start.5 = (f32[9,16,128]{2,1,0:T(8,128)S(1)}, f32[9,16,128]{2,1,0:T(8,128)S(1)}, u32[]{:S(2)}, u32[]{:S(2)}) collective-permute-start(f32[9,16,128]{2,1,0:T(8,128)S(1)} %get-tuple-element.34), channel_id=1, source_target_pairs={{0,3},{1,0},{2,1},{3,2},{4,7},{5,4},{6,5},{7,6},{8,11},{9,8},{10,9... | collective-permute-start | bytes 221192 | tf_op jit(solution)/shard_map/ppermute | solution.py:194
  43.5 15.7 %collective-permute-start.6 = (f32[32,16,128]{2,1,0:T(8,128)S(1)}, f32[32,16,128]{2,1,0:T(8,128)S(1)}, u32[]{:S(2)}, u32[]{:S(2)}) collective-permute-start(f32[32,16,128]{2,1,0:T(8,128)S(1)} %get-tuple-element.36), channel_id=1, source_target_pairs={{0,32},{32,64},{64,96},{96,0},{1,33},{33,65},{65,97},{97,1},{2,34}... | collective-permute-start | bytes 786440 | tf_op jit(solution)/shard_map/ppermute | solution.py:193
  43.5 15.7 %collective-permute-start.7 = (f32[32,16,128]{2,1,0:T(8,128)S(1)}, f32[32,16,128]{2,1,0:T(8,128)S(1)}, u32[]{:S(2)}, u32[]{:S(2)}) collective-permute-start(f32[32,16,128]{2,1,0:T(8,128)S(1)} %get-tuple-element.37), channel_id=1, source_target_pairs={{0,96},{32,0},{64,32},{96,64},{1,97},{33,1},{65,33},{97,65},{2,98}... | collective-permute-start | bytes 786440 | tf_op jit(solution)/shard_map/ppermute | solution.py:194
  46.2 13.0 %collective-permute-start.8 = (f32[32,16,128]{2,1,0:T(8,128)S(1)}, f32[32,16,128]{2,1,0:T(8,128)S(1)}, u32[]{:S(2)}, u32[]{:S(2)}) collective-permute-start(f32[32,16,128]{2,1,0:T(8,128)S(1)} %get-tuple-element.38), channel_id=1, source_target_pairs={{0,4},{4,8},{8,12},{12,16},{16,20},{20,24},{24,28},{28,0},{1,5},{5... | collective-permute-start | bytes 786440 | tf_op jit(solution)/shard_map/ppermute | solution.py:193
  46.2 13.0 %collective-permute-start.9 = (f32[32,16,128]{2,1,0:T(8,128)S(1)}, f32[32,16,128]{2,1,0:T(8,128)S(1)}, u32[]{:S(2)}, u32[]{:S(2)}) collective-permute-start(f32[32,16,128]{2,1,0:T(8,128)S(1)} %get-tuple-element.39), channel_id=1, source_target_pairs={{0,28},{4,0},{8,4},{12,8},{16,12},{20,16},{24,20},{28,24},{1,29},{... | collective-permute-start | bytes 786440 | tf_op jit(solution)/shard_map/ppermute | solution.py:194
  49.8 8.1 %collective-permute-start.11 = (f32[8,16,128]{2,1,0:T(8,128)S(1)}, f32[8,16,128]{2,1,0:T(8,128)S(1)}, u32[]{:S(2)}, u32[]{:S(2)}) collective-permute-start(f32[8,16,128]{2,1,0:T(8,128)S(1)} %get-tuple-element.40), channel_id=1, source_target_pairs={{0,3},{1,0},{2,1},{3,2},{4,7},{5,4},{6,5},{7,6},{8,11},{9,8},{10,9... | collective-permute-start | bytes 196616 | tf_op jit(solution)/shard_map/ppermute | solution.py:194
  66.4 15.1 %collective-permute-start.12 = (f32[16,16,128]{2,1,0:T(8,128)S(1)}, f32[16,16,128]{2,1,0:T(8,128)S(1)}, u32[]{:S(2)}, u32[]{:S(2)}) collective-permute-start(f32[16,16,128]{2,1,0:T(8,128)S(1)} %get-tuple-element.42), channel_id=1, source_target_pairs={{0,32},{32,64},{64,96},{96,0},{1,33},{33,65},{65,97},{97,1},{2,34}... | collective-permute-start | bytes 393224 | tf_op jit(solution)/shard_map/ppermute | solution.py:193
  66.5 15.0 %collective-permute-start.13 = (f32[16,16,128]{2,1,0:T(8,128)S(1)}, f32[16,16,128]{2,1,0:T(8,128)S(1)}, u32[]{:S(2)}, u32[]{:S(2)}) collective-permute-start(f32[16,16,128]{2,1,0:T(8,128)S(1)} %get-tuple-element.43), channel_id=1, source_target_pairs={{0,96},{32,0},{64,32},{96,64},{1,97},{33,1},{65,33},{97,65},{2,98}... | collective-permute-start | bytes 393224 | tf_op jit(solution)/shard_map/ppermute | solution.py:194
  69.1 12.4 %collective-permute-start.14 = (f32[16,16,128]{2,1,0:T(8,128)S(1)}, f32[16,16,128]{2,1,0:T(8,128)S(1)}, u32[]{:S(2)}, u32[]{:S(2)}) collective-permute-start(f32[16,16,128]{2,1,0:T(8,128)S(1)} %get-tuple-element.44), channel_id=1, source_target_pairs={{0,4},{4,8},{8,12},{12,16},{16,20},{20,24},{24,28},{28,0},{1,5},{5... | collective-permute-start | bytes 393224 | tf_op jit(solution)/shard_map/ppermute | solution.py:193
  69.1 12.4 %collective-permute-start.15 = (f32[16,16,128]{2,1,0:T(8,128)S(1)}, f32[16,16,128]{2,1,0:T(8,128)S(1)}, u32[]{:S(2)}, u32[]{:S(2)}) collective-permute-start(f32[16,16,128]{2,1,0:T(8,128)S(1)} %get-tuple-element.45), channel_id=1, source_target_pairs={{0,28},{4,0},{8,4},{12,8},{16,12},{20,16},{24,20},{28,24},{1,29},{... | collective-permute-start | bytes 393224 | tf_op jit(solution)/shard_map/ppermute | solution.py:194
  72.7 7.6 %collective-permute-start.17 = (f32[4,16,128]{2,1,0:T(8,128)S(1)}, f32[4,16,128]{2,1,0:T(8,128)S(1)}, u32[]{:S(2)}, u32[]{:S(2)}) collective-permute-start(f32[4,16,128]{2,1,0:T(8,128)S(1)} %get-tuple-element.46), channel_id=1, source_target_pairs={{0,3},{1,0},{2,1},{3,2},{4,7},{5,4},{6,5},{7,6},{8,11},{9,8},{10,9... | collective-permute-start | bytes 98312 | tf_op jit(solution)/shard_map/ppermute | solution.py:194
  87.6 13.9 %collective-permute-start.18 = (f32[16,16,128]{2,1,0:T(8,128)S(1)}, f32[16,16,128]{2,1,0:T(8,128)S(1)}, u32[]{:S(2)}, u32[]{:S(2)}) collective-permute-start(f32[16,16,128]{2,1,0:T(8,128)S(1)} %get-tuple-element.48), channel_id=1, source_target_pairs={{0,32},{32,64},{64,96},{96,0},{1,33},{33,65},{65,97},{97,1},{2,34}... | collective-permute-start | bytes 393224 | tf_op jit(solution)/shard_map/ppermute | solution.py:193
  87.6 13.9 %collective-permute-start.19 = (f32[16,16,128]{2,1,0:T(8,128)S(1)}, f32[16,16,128]{2,1,0:T(8,128)S(1)}, u32[]{:S(2)}, u32[]{:S(2)}) collective-permute-start(f32[16,16,128]{2,1,0:T(8,128)S(1)} %get-tuple-element.49), channel_id=1, source_target_pairs={{0,96},{32,0},{64,32},{96,64},{1,97},{33,1},{65,33},{97,65},{2,98}... | collective-permute-start | bytes 393224 | tf_op jit(solution)/shard_map/ppermute | solution.py:194
  90.3 11.2 %collective-permute-start.20 = (f32[16,16,128]{2,1,0:T(8,128)S(1)}, f32[16,16,128]{2,1,0:T(8,128)S(1)}, u32[]{:S(2)}, u32[]{:S(2)}) collective-permute-start(f32[16,16,128]{2,1,0:T(8,128)S(1)} %get-tuple-element.50), channel_id=1, source_target_pairs={{0,4},{4,8},{8,12},{12,16},{16,20},{20,24},{24,28},{28,0},{1,5},{5... | collective-permute-start | bytes 393224 | tf_op jit(solution)/shard_map/ppermute | solution.py:193
  90.3 11.2 %collective-permute-start.21 = (f32[16,16,128]{2,1,0:T(8,128)S(1)}, f32[16,16,128]{2,1,0:T(8,128)S(1)}, u32[]{:S(2)}, u32[]{:S(2)}) collective-permute-start(f32[16,16,128]{2,1,0:T(8,128)S(1)} %get-tuple-element.51), channel_id=1, source_target_pairs={{0,28},{4,0},{8,4},{12,8},{16,12},{20,16},{24,20},{28,24},{1,29},{... | collective-permute-start | bytes 393224 | tf_op jit(solution)/shard_map/ppermute | solution.py:194
  93.9 6.4 %collective-permute-start.23 = (f32[4,16,128]{2,1,0:T(8,128)S(1)}, f32[4,16,128]{2,1,0:T(8,128)S(1)}, u32[]{:S(2)}, u32[]{:S(2)}) collective-permute-start(f32[4,16,128]{2,1,0:T(8,128)S(1)} %get-tuple-element.52), channel_id=1, source_target_pairs={{0,3},{1,0},{2,1},{3,2},{4,7},{5,4},{6,5},{7,6},{8,11},{9,8},{10,9... | collective-permute-start | bytes 98312 | tf_op jit(solution)/shard_map/ppermute | solution.py:194
  116.5 4.5 %collective-permute-start.26 = (f32[80,128]{1,0:T(8,128)S(1)}, f32[80,128]{1,0:T(8,128)S(1)}, u32[]{:S(2)}, u32[]{:S(2)}) collective-permute-start(f32[80,128]{1,0:T(8,128)S(1)} %get-tuple-element.53), channel_id=1, source_target_pairs={{0,96},{32,64},{64,32},{96,0},{1,97},{33,65},{65,33},{97,1},{2,98}... | collective-permute-start | bytes 122888 | tf_op jit(solution)/shard_map/ppermute | solution.py:246
  116.5 4.5 %collective-permute-start.25 = (f32[80,128]{1,0:T(8,128)S(1)}, f32[80,128]{1,0:T(8,128)S(1)}, u32[]{:S(2)}, u32[]{:S(2)}) collective-permute-start(f32[80,128]{1,0:T(8,128)S(1)} %get-tuple-element.53), channel_id=1, source_target_pairs={{0,64},{32,96},{64,0},{96,32},{1,65},{33,97},{65,1},{97,33},{2,66}... | collective-permute-start | bytes 122888 | tf_op jit(solution)/shard_map/ppermute | solution.py:246
  116.9 4.7 %collective-permute-start.24 = (f32[80,128]{1,0:T(8,128)S(1)}, f32[80,128]{1,0:T(8,128)S(1)}, u32[]{:S(2)}, u32[]{:S(2)}) collective-permute-start(f32[80,128]{1,0:T(8,128)S(1)} %get-tuple-element.53), channel_id=1, source_target_pairs={{0,32},{32,0},{64,96},{96,64},{1,33},{33,1},{65,97},{97,65},{2,34}... | collective-permute-start | bytes 122888 | tf_op jit(solution)/shard_map/ppermute | solution.py:246
  121.6 6.8 %collective-permute-start.29 = (f32[80,128]{1,0:T(8,128)S(1)}, f32[80,128]{1,0:T(8,128)S(1)}, u32[]{:S(2)}, u32[]{:S(2)}) collective-permute-start(f32[80,128]{1,0:T(8,128)S(1)} %add_add_fusion.1), channel_id=1, source_target_pairs={{0,3},{1,2},{2,1},{3,0},{4,7},{5,6},{6,5},{7,4},{8,11},{9,10},{10,... | collective-permute-start | bytes 122888 | tf_op jit(solution)/shard_map/ppermute | solution.py:246
  (17 other events, 128.6 us)
